TPU v7x, 256 devices: a whole 4x4x8 slice. The times are simulated.
256 devices in a mesh: mem: 16 (over y, x), space: 16 (over z, core).
Axes of the slice: x: 4, y: 4, z: 8, core: 2. Of those that a mesh axis runs over, the one named last changes fastest.
Arguments:
- ensemble: bfloat16 [64, 16, 184320], P('mem', None, 'space'), may hold values from -100 to 100
- cotangent: bfloat16 [64, 16, 184320], P('mem', None, 'space'), may hold values from -6 to 6
- w_query: bfloat16 [16, 16], replicated, may hold values from -2 to 2
- w_key: bfloat16 [16, 16], replicated, may hold values from -2 to 2
- w_value: bfloat16 [16, 16], replicated, may hold values from -1.5 to 1.5
- w_out: bfloat16 [16, 16], replicated, may hold values from -1.5 to 1.5
Outputs:
- updated: float32 [64, 16, 184320], P('mem', None, 'space')
- ensemble_grad: float32 [64, 16, 184320], P('mem', None, 'space')
All inputs are finite; a program needn't handle non-finite values.
Results may differ from a plain program's by a relative error of at most 0.0044.
Values may be sent and summed in bfloat16 or wider, within the bound.
A program may use at most 128 MiB of HBM per device.

v0:
```python
import functools
import math

import jax
import jax.numpy as jnp
from jax import lax
from jax.sharding import Mesh
from jax.sharding import PartitionSpec as P

MEM = ("mem_0", "mem_1")
SPACE = ("space_0", "space_1")
MEM_SPACE = ("mem_0", "mem_1", "space_0", "space_1")


def side_by_side(arrays, axis, split_dim, concat_dim, along):
    both = jnp.concatenate(arrays, axis=along)
    out, at, done = (
        lax.all_to_all(both, axis, split_axis=split_dim, concat_axis=concat_dim, tiled=True),
        0,
        [],
    )
    for a in arrays:
        done.append(lax.slice_in_dim(out, at, at + a.shape[along], axis=along))
        at += a.shape[along]
    return tuple(done)


def over_axes(value, axes):
    return functools.reduce(lax.psum, axes, value)


def project(weight, field):
    return jnp.einsum("cd,mdp->mcp", weight, field, preferred_element_type=jnp.float32)


def project_back(weight, field):
    return jnp.einsum("cd,mcp->mdp", weight, field, preferred_element_type=jnp.float32)


def flatten(field):
    return field.reshape(field.shape[0], field.shape[1] * field.shape[2])


def pair_sum(left, right):
    return lax.dot_general(
        flatten(left), flatten(right), (((1,), (1,)), ((), ())), preferred_element_type=jnp.float32
    )


def normalize(scores):
    row_peak = jnp.max(scores, axis=1, keepdims=True)
    exponent = jnp.exp(scores - row_peak)
    return exponent / jnp.sum(exponent, axis=1, keepdims=True)


def combine(weights_half, field):
    mixed = jnp.dot(weights_half, flatten(field), preferred_element_type=jnp.float32)
    return mixed.astype(jnp.bfloat16).reshape(field.shape)


def shards(ensemble, cotangent, w_query, w_key, w_value, w_out):
    mem_count = lax.axis_size(MEM)
    space_count = lax.axis_size(SPACE)
    fields, grad_fields = side_by_side((ensemble, cotangent), MEM, 2, 0, 1)
    members, channels, cell_count = fields.shape
    score_scale = 1.0 / (cell_count * mem_count * space_count * math.sqrt(channels))
    queries = project(w_query, fields).astype(jnp.bfloat16)
    key_field = project(w_key, fields).astype(jnp.bfloat16)
    value_field = project(w_value, fields).astype(jnp.bfloat16)
    partial_scores = pair_sum(queries, key_field)
    grad_mixed = project_back(w_out, grad_fields).astype(jnp.bfloat16)
    partial_pairs = pair_sum(grad_mixed, value_field)
    total_scores, total_pairs = (
        over_axes(partial_scores, MEM_SPACE),
        over_axes(partial_pairs, MEM_SPACE),
    )
    weights = normalize(score_scale * total_scores)
    weights_half = weights.astype(jnp.bfloat16)
    mixed = combine(weights_half, value_field)
    branch = project(w_out, mixed).astype(jnp.bfloat16)
    grad_scores = weights * (total_pairs - jnp.sum(weights * total_pairs, axis=1, keepdims=True))
    grad_scaled = (score_scale * grad_scores).astype(jnp.bfloat16)
    grad_queries = combine(grad_scaled, key_field)
    grad_keys = combine(grad_scaled.T, queries)
    grad_values = combine(weights_half.T, grad_mixed)
    grad_branch = (
        project_back(w_query, grad_queries)
        + project_back(w_key, grad_keys)
        + project_back(w_value, grad_values)
    ).astype(jnp.bfloat16)
    branch_home, grad_home = side_by_side((branch, grad_branch), MEM, 0, 2, 1)
    updated = ensemble.astype(jnp.float32) + branch_home.astype(jnp.float32)
    ensemble_grad = cotangent.astype(jnp.float32) + grad_home.astype(jnp.float32)
    return (updated, ensemble_grad)


def solution(mesh):
    torus = Mesh(mesh.devices.reshape(4, 4, 8, 2), ("mem_0", "mem_1", "space_0", "space_1"))
    placed = (P(MEM, None, SPACE), P(MEM, None, SPACE), P(), P(), P(), P())
    return jax.shard_map(
        shards,
        mesh=torus,
        in_specs=placed,
        out_specs=(P(MEM, None, SPACE), P(MEM, None, SPACE)),
        check_vma=False,
    )
```

profile of v0, /device:TPU:1, one launch (start us, length us, event | category | flops | bytes accessed | tf_op | source)
XLA Modules:
  0.0 286.1 jit_solution(9159615233748137519)
XLA Ops:
  0.6 2.0 pad_maximum_fusion.1
  2.7 10.9 %copy.30 = bf16[4,32,11520]{1,0,2:T(4,128)(2,1)} copy(bf16[4,32,11520]{2,1,0:T(8,128)(2,1)S(1)} %pad_maximum_fusion.1) | data formatting | bytes 5898240 | tf_op jit(solution)/shard_map/concatenate | solution.py:16
  13.6 15.5 %reshape.53 = bf16[16,2,46080]{2,1,0:T(2,128)(2,1)S(1)} reshape(bf16[11520,4,32]{2,1,0:T(4,128)(2,1)} %bitcast.59) | data formatting | bytes 5898240
  29.1 44.2 %all_to_all.36 = bf16[16,2,46080]{2,1,0:T(2,128)(2,1)} all-to-all(bf16[16,2,46080]{2,1,0:T(2,128)(2,1)S(1)} %reshape.53), channel_id=1, replica_groups=mesh['mem_0'=4,'mem_1'=4,'space_0'=8,'space_1'=2] {'mem_0','mem_1'}, dimensions={0} | all-to-all | bytes 5898240 | tf_op jit(solution)/shard_map/all_to_all | solution.py:18
  73.3 14.4 %reshape.54 = bf16[11520,4,32]{2,1,0:T(4,128)(2,1)} reshape(bf16[16,2,46080]{2,1,0:T(2,128)(2,1)} %all_to_all.36) | data formatting | bytes 5898240
  87.7 15.4 %copy.31 = bf16[4,32,16,720]{3,1,0,2:T(8,128)(2,1)S(1)} copy(bf16[4,32,16,720]{1,0,3,2:T(4,128)(2,1)} %bitcast.60) | data formatting | bytes 5898240 | tf_op jit(solution)/shard_map/all_to_all | solution.py:18
  103.1 1.7 fusion.11
  104.8 4.3 %reshape.37 = bf16[64,11520]{1,0:T(8,128)(2,1)} reshape(bf16[64,16,720]{2,1,0:T(8,128)(2,1)} %fusion.11) | data formatting | bytes 2949120 | tf_op jit(solution)/shard_map/reshape | solution.py:41
  109.6 1.1 copy-done.3
  110.8 1.7 fusion.18
  112.5 4.3 %reshape.39 = bf16[64,11520]{1,0:T(8,128)(2,1)} reshape(bf16[64,16,720]{2,1,0:T(8,128)(2,1)} %copy-done.3) | data formatting | bytes 2949120 | tf_op jit(solution)/shard_map/reshape | solution.py:41
  116.8 1.8 fusion.7
  118.6 1.7 fusion.12
  120.3 3.5 %reshape.41 = bf16[64,11520]{1,0:T(8,128)(2,1)S(1)} reshape(bf16[64,16,720]{2,1,0:T(8,128)(2,1)} %fusion.7) | data formatting | bytes 2949120 | tf_op jit(solution)/shard_map/reshape | solution.py:41
  123.8 3.1 %fusion.23 = f32[64,64]{1,0:T(8,128)S(1)} fusion(bf16[64,16,720]{2,1,0:T(8,128)(2,1)S(1)} %copy-done.1, bf16[64,16,720]{2,1,0:T(8,128)(2,1)} %fusion.7), kind=kOutput, calls=%fused_computation.31 | convolution fusion | flops 94371840 | bytes 2965504 | tf_op jit(solution)/shard_map/dot_general | solution.py:45
  126.9 3.3 %reshape.35 = bf16[64,11520]{1,0:T(8,128)(2,1)} reshape(bf16[64,16,720]{2,1,0:T(8,128)(2,1)S(1)} %copy-done.1) | data formatting | bytes 2949120 | tf_op jit(solution)/shard_map/reshape | solution.py:41
  130.2 12.0 %all-reduce.2 = (f32[64,64]{1,0:T(8,128)S(1)}, f32[64,64]{1,0:T(8,128)S(1)}) all-reduce(f32[64,64]{1,0:T(8,128)S(1)} %fusion.18, f32[64,64]{1,0:T(8,128)S(1)} %fusion.23), channel_id=1, replica_groups=mesh['mem_0'=4,'mem_1'=4,'space_0'=8,'space_1'=2] {'mem_0'}, use_global_device_ids=true, to_apply=%region_0.0 | all-reduce | flops 8192 | bytes 65536 | tf_op jit(solution)/shard_map/psum | solution.py:29
  142.2 12.1 %all-reduce.1 = (f32[64,64]{1,0:T(8,128)S(1)}, f32[64,64]{1,0:T(8,128)S(1)}) all-reduce(f32[64,64]{1,0:T(8,128)S(1)} %get-tuple-element.6, f32[64,64]{1,0:T(8,128)S(1)} %get-tuple-element.7), channel_id=1, replica_groups=mesh['mem_0'=4,'mem_1'=4,'space_0'=8,'space_1'=2] {'mem_1'}, use_global_device_ids=true, to_apply=%region_1.0 | all-reduce | flops 8192 | bytes 65536 | tf_op jit(solution)/shard_map/psum | solution.py:29
  154.3 26.2 %all-reduce = (f32[64,64]{1,0:T(8,128)S(1)}, f32[64,64]{1,0:T(8,128)S(1)}) all-reduce(f32[64,64]{1,0:T(8,128)S(1)} %get-tuple-element.4, f32[64,64]{1,0:T(8,128)S(1)} %get-tuple-element.5), channel_id=1, replica_groups=mesh['mem_0'=4,'mem_1'=4,'space_0'=8,'space_1'=2] {'space_0'}, use_global_device_ids=true, to_apply=%region_2.0 | all-reduce | flops 8192 | bytes 65536 | tf_op jit(solution)/shard_map/psum | solution.py:29
  180.6 19.7 %all-reduce.3 = (f32[64,64]{1,0:T(8,128)S(1)}, f32[64,64]{1,0:T(8,128)S(1)}) all-reduce(f32[64,64]{1,0:T(8,128)S(1)} %get-tuple-element.2, f32[64,64]{1,0:T(8,128)S(1)} %get-tuple-element.3), channel_id=1, replica_groups=mesh['mem_0'=4,'mem_1'=4,'space_0'=8,'space_1'=2] {'space_1'}, use_global_device_ids=true, to_apply=%region_3.0 | all-reduce | flops 8192 | bytes 65536 | tf_op jit(solution)/shard_map/psum | solution.py:29
  200.6 1.8 convolution_convert_fusion
  202.4 1.7 convolution_convert_fusion.3
  205.5 1.7 convolution_convert_fusion.2
  207.2 4.3 %reshape.38 = bf16[64,16,720]{2,1,0:T(8,128)(2,1)S(1)} reshape(bf16[64,11520]{1,0:T(8,128)(2,1)} %convolution_convert_fusion.2) | data formatting | bytes 2949120 | tf_op jit(solution)/shard_map/reshape | solution.py:58
  211.5 4.0 %reshape.40 = bf16[64,16,720]{2,1,0:T(8,128)(2,1)} reshape(bf16[64,11520]{1,0:T(8,128)(2,1)S(1)} %convolution_convert_fusion.1) | data formatting | bytes 2949120 | tf_op jit(solution)/shard_map/reshape | solution.py:58
  215.5 4.3 %reshape.36 = bf16[64,16,720]{2,1,0:T(8,128)(2,1)S(1)} reshape(bf16[64,11520]{1,0:T(8,128)(2,1)} %convolution_convert_fusion.3) | data formatting | bytes 2949120 | tf_op jit(solution)/shard_map/reshape | solution.py:58
  219.8 1.7 fusion.13
  221.5 5.1 %reshape.42 = bf16[64,16,720]{2,1,0:T(8,128)(2,1)} reshape(bf16[64,11520]{1,0:T(8,128)(2,1)} %convolution_convert_fusion) | data formatting | bytes 2949120 | tf_op jit(solution)/shard_map/reshape | solution.py:58
  230.6 42.2 %all_to_all.37 = bf16[64,32,720]{2,1,0:T(8,128)(2,1)S(1)} all-to-all(bf16[64,32,720]{2,1,0:T(8,128)(2,1)S(1)} %pad_maximum_fusion), channel_id=1, replica_groups=mesh['mem_0'=4,'mem_1'=4,'space_0'=8,'space_1'=2] {'mem_0','mem_1'}, dimensions={0} | all-to-all | bytes 5898240 | tf_op jit(solution)/shard_map/all_to_all | solution.py:18
  272.8 1.8 copy.40
  274.5 5.7 %all_to_all.33 = bf16[4,32,11520]{2,1,0:T(8,128)(2,1)} reshape(bf16[4,32,16,720]{3,2,1,0:T(8,128)(2,1)S(1)} %copy.40) | data formatting | bytes 5898240 | tf_op jit(solution)/shard_map/all_to_all | solution.py:18
  280.2 5.8 %convert_add_fusion = (f32[4,16,11520]{2,1,0:T(8,128)}, f32[4,16,11520]{2,1,0:T(8,128)}) fusion(bf16[4,16,11520]{2,1,0:T(8,128)(2,1)} %param.7, bf16[4,32,11520]{2,1,0:T(8,128)(2,1)} %all_to_all.33, bf16[4,16,11520]{2,1,0:T(8,128)(2,1)} %param.6), kind=kLoop, calls=%fused_computation.7 | loop fusion | flops 4423680 | bytes 11796480 | tf_op jit(solution)/shard_map/add | solution.py:93
  (34 shorter events, 6.2 us)
Async XLA Ops:
  0.6 116.2 %copy-start = (bf16[16,16]{1,0:T(8,128)(2,1)S(1)}, bf16[16,16]{1,0:T(8,128)(2,1)}, u32[]{:S(2)}) copy-start(bf16[16,16]{1,0:T(8,128)(2,1)} %param.11) | copy-start | bytes 1540
  87.7 15.4 %copy-start.11 = (bf16[16,16]{1,0:T(8,128)(2,1)S(1)}, bf16[16,16]{1,0:T(8,128)(2,1)}, u32[]{:S(2)}) copy-start(bf16[16,16]{1,0:T(8,128)(2,1)} %param.9) | copy-start | bytes 1540
  104.8 4.3 %copy-start.12 = (bf16[16,16]{1,0:T(8,128)(2,1)S(1)}, bf16[16,16]{1,0:T(8,128)(2,1)}, u32[]{:S(2)}) copy-start(bf16[16,16]{1,0:T(8,128)(2,1)} %param.8) | copy-start | bytes 1540
  109.1 1.7 copy-start.2
  109.6 1.1 copy-start.3
  116.8 1.8 copy-start.10
  120.3 3.5 %copy-start.1 = (bf16[64,16,720]{2,1,0:T(8,128)(2,1)S(1)}, bf16[64,16,720]{2,1,0:T(8,128)(2,1)}, u32[]{:S(2)}) copy-start(bf16[64,16,720]{2,1,0:T(8,128)(2,1)} %fusion.12) | copy-start | bytes 4423684
  180.5 21.8 %copy-start.9 = (bf16[64,11520]{1,0:T(8,128)(2,1)S(1)}, bf16[64,11520]{1,0:T(8,128)(2,1)}, u32[]{:S(2)}) copy-start(bf16[64,11520]{1,0:T(8,128)(2,1)} %reshape.35) | copy-start | bytes 4423684
  202.4 1.9 copy-start.8
  204.1 1.4 copy-start.7
  221.5 5.1 %copy-start.5 = (bf16[64,16,720]{2,1,0:T(8,128)(2,1)S(1)}, bf16[64,16,720]{2,1,0:T(8,128)(2,1)}, u32[]{:S(2)}) copy-start(bf16[64,16,720]{2,1,0:T(8,128)(2,1)} %reshape.40) | copy-start | bytes 4423684
  227.2 1.4 copy-start.6
  228.7 1.4 copy-start.4
where the time goes:
time: 288 us; the launch traced here: 286 us
  blocking collectives  156 us (54%)
  local copies, waits for them, and re-layouts  99.6 us (35%)
  matrix products  20.4 us (7%)
  other arithmetic  8.86 us (3%)
    all_to_all x2, blocking collectives, side_by_side(): lax.all_to_all(both, axis, split_axis=split_dim, concat_axis=concat_dim,...  86.4 us
    psum x4, blocking collectives, over_axes(): return functools.reduce(lax.psum, axes, value)  70.1 us
    unnamed x28, local copies, waits for them, and re-layouts  32.8 us
    all_to_all x3, local copies, waits for them, and re-layouts, side_by_side(): lax.all_to_all(both, axis, split_axis=split_dim, concat_axis=concat_dim,...  22.8 us
    reshape x4, local copies, waits for them, and re-layouts, combine(): return mixed.astype(jnp.bfloat16).reshape(field.shape)  17.7 us
    reshape x4, local copies, waits for them, and re-layouts, flatten(): return field.reshape(field.shape[0], field.shape[1] * field.shape[2])  15.3 us
    concatenate x1, local copies, waits for them, and re-layouts, side_by_side(): both = jnp.concatenate(arrays, axis=along)  10.9 us
    dot_general x4, matrix products, combine(): jnp.dot(weights_half, flatten(field), preferred_element_type=jnp.float32)  5.92 us

commit v1 on v0

v1 whole, which is shorter than its diff:
```python
import functools
import math

import jax
import jax.numpy as jnp
from jax import lax
from jax.experimental import pallas as pl
from jax.experimental.pallas import tpu as pltpu
from jax.sharding import Mesh
from jax.sharding import PartitionSpec as P

MESH = pl.DeviceIdType.MESH
F32 = jnp.float32
BF16 = jnp.bfloat16
HIGH = lax.Precision.HIGHEST

NX, NY, NZ, NC = 4, 4, 8, 2
PEERS = NX * NY
CH = 16
MEM_DEV = 4
ROWS = MEM_DEV * CH
MEMBERS = MEM_DEV * PEERS
ALL = ROWS * PEERS
TILE = 128
MAIN = 5
EXTRA = 10
WIDTH = (MAIN + 1) * TILE
CELL_DEV = 11520
CHUNKS = ((0, 256), (256, 256), (512, 128))
XLO = MAIN * TILE
HOPS = (1, 3, 2)


def nt(a, b, precision=None):
    return lax.dot_general(
        a, b, (((1,), (1,)), ((), ())), precision=precision, preferred_element_type=F32
    )


def tn(a, b, precision=None):
    return lax.dot_general(
        a, b, (((0,), (0,)), ((), ())), precision=precision, preferred_element_type=F32
    )


def hop(i):
    return 2 - i + 3 * (i // 2) + 2 * (i // 3)


def kernel(
    scale,
    e_hbm,
    c_hbm,
    wq_ref,
    wk_ref,
    wv_ref,
    wo_ref,
    ob,
    og,
    re1,
    rc1,
    e_all,
    c_all,
    bm,
    gm,
    rb,
    rg,
    sacc,
    pacc,
    consts,
    sfull,
    cbuf,
    ysrc,
    ybuf,
    xsrc,
    xbuf,
    zsrc,
    zbuf,
    sfin,
    wexp,
    wtexp,
    gexp,
    gtexp,
    dblk,
    gblk,
    tblk,
    s1_send,
    s1_recv,
    s1x_send,
    s1x_recv,
    s2_send,
    s2_recv,
    s2x_send,
    s2x_recv,
    c_sem,
    y_sem,
    x_sem,
    z_sem,
    f_sem,
    q1_send,
    q1_recv,
    q1x_send,
    q1x_recv,
    q2_send,
    q2x_send,
    o_recv,
):
    y, x = lax.axis_index("y"), lax.axis_index("x")
    z, c = lax.axis_index("z"), lax.axis_index("c")

    def at(dy=0, dx=0, dz=0, dc=0):
        return (
            lax.rem(y + dy, NY),
            lax.rem(x + dx, NX),
            lax.rem(z + dz, NZ),
            lax.rem(c + dc, NC),
        )

    def order(yd, xd):
        return 4 * lax.rem(xd + yd + 2 * c, 4) + yd

    def lanes(yd, xd, lo, width):
        return pl.ds(pl.multiple_of((4 * yd + xd) * XLO + lo, TILE), width)

    def extra_lanes(yd, xd):
        return pl.ds(pl.multiple_of((MAIN * PEERS + order(yd, xd)) * TILE, TILE), TILE)

    def remote(src, dst, send, recv, device):
        pltpu.make_async_remote_copy(
            src_ref=src, dst_ref=dst, send_sem=send, recv_sem=recv, device_id=device, device_id_type=MESH
        ).start()

    def local(src, dst, sem):
        pltpu.make_async_copy(src, dst, sem).start()

    def await_bytes(view, sem):
        pltpu.make_async_copy(view, view, sem).wait()

    barrier = pltpu.get_barrier_semaphore()
    partners = [at(dc=1)]
    partners += [at(dy=d) for d in (1, 2, 3)] + [at(dx=d) for d in (1, 2, 3)]
    partners += [at(dz=d) for d in range(1, NZ)]
    for device in partners:
        pl.semaphore_signal(barrier, inc=1, device_id=device, device_id_type=MESH)
    pl.semaphore_wait(barrier, len(partners))

    for j, (lo, width) in enumerate(CHUNKS):
        for d in HOPS:

            @pl.loop(0, 4)
            def _(k, j=j, lo=lo, width=width, d=d):
                xd, yd = lax.rem(x + d, 4), lax.rem(y + d, 4)
                part = pl.ds(lo, width)
                remote(
                    e_hbm.at[:, lanes(k, xd, lo, width)],
                    re1.at[k, x, :, part],
                    s1_send.at[0],
                    s1_recv.at[0, j],
                    at(dx=d),
                )
                remote(
                    c_hbm.at[:, lanes(yd, k, lo, width)],
                    rc1.at[k, y, :, part],
                    s1_send.at[1],
                    s1_recv.at[1, j],
                    at(dy=d),
                )

        @pl.loop(0, 4)
        def _(k, j=j, lo=lo, width=width):
            part = pl.ds(lo, width)
            local(e_hbm.at[:, lanes(k, x, lo, width)], re1.at[k, x, :, part], s1_recv.at[0, j])
            local(c_hbm.at[:, lanes(y, k, lo, width)], rc1.at[k, y, :, part], s1_recv.at[1, j])

    last = pl.ds(XLO, TILE)
    for d in HOPS:

        @pl.loop(0, 4)
        def _(k, d=d):
            xd, yd = lax.rem(x + d, 4), lax.rem(y + d, 4)

            @pl.when(order(k, xd) < EXTRA)
            def _():
                remote(
                    e_hbm.at[:, extra_lanes(k, xd)],
                    re1.at[k, x, :, last],
                    s1x_send.at[0, d, k],
                    s1x_recv.at[0, k],
                    at(dx=d),
                )

            @pl.when(order(yd, k) < EXTRA)
            def _():
                remote(
                    c_hbm.at[:, extra_lanes(yd, k)],
                    rc1.at[k, y, :, last],
                    s1x_send.at[1, d, k],
                    s1x_recv.at[1, k],
                    at(dy=d),
                )

    @pl.loop(0, 4)
    def _(k):
        @pl.when(order(k, x) < EXTRA)
        def _():
            local(e_hbm.at[:, extra_lanes(k, x)], re1.at[k, x, :, last], s1x_recv.at[0, k])

        @pl.when(order(y, k) < EXTRA)
        def _():
            local(c_hbm.at[:, extra_lanes(y, k)], rc1.at[k, y, :, last], s1x_recv.at[1, k])

    @pl.when(order(y, x) >= EXTRA)
    def _():
        e_all[:, :, :, XLO:] = jnp.zeros((4, 4, ROWS, TILE), BF16)
        c_all[:, :, :, XLO:] = jnp.zeros((4, 4, ROWS, TILE), BF16)

    sacc[...] = jnp.zeros_like(sacc)
    pacc[...] = jnp.zeros_like(pacc)
    a_mat = tn(wq_ref[...], wk_ref[...])
    at_mat = tn(wk_ref[...], wq_ref[...])
    m_mat = jnp.dot(wo_ref[...], wv_ref[...], preferred_element_type=F32)
    mt_mat = lax.dot_general(
        wv_ref[...], wo_ref[...], (((0,), (1,)), ((), ())), preferred_element_type=F32
    )
    row16 = lax.broadcasted_iota(jnp.int32, (CH, 256), 0)
    lane16 = lax.rem(lax.broadcasted_iota(jnp.int32, (CH, 256), 1), CH)
    repeat = (row16 == lane16).astype(F32)
    for i, mat in enumerate((a_mat, at_mat, m_mat, mt_mat)):
        consts[i] = jnp.dot(mat, repeat, precision=HIGH, preferred_element_type=F32)

    for j, (lo, width) in enumerate(CHUNKS):
        part = pl.ds(lo, width)
        await_bytes(re1.at[:, :, :, part], s1_recv.at[0, j])
        await_bytes(rc1.at[:, :, :, part], s1_recv.at[1, j])
        for d in HOPS:
            yd, xd = lax.rem(y + d, 4), lax.rem(x + d, 4)
            remote(re1.at[yd, :, :, part], e_all.at[y, :, :, part], s2_send.at[0], s2_recv.at[0, j], at(dy=d))
            remote(rc1.at[xd, :, :, part], c_all.at[:, x, :, part], s2_send.at[1], s2_recv.at[1, j], at(dx=d))
        local(re1.at[y, :, :, part], e_all.at[y, :, :, part], s2_recv.at[0, j])
        local(rc1.at[x, :, :, part], c_all.at[:, x, :, part], s2_recv.at[1, j])

    for k in range(4):

        @pl.when(order(k, x) < EXTRA)
        def _(k=k):
            await_bytes(re1.at[k, :, :, last], s1x_recv.at[0, k])

        @pl.when(order(y, k) < EXTRA)
        def _(k=k):
            await_bytes(rc1.at[k, :, :, last], s1x_recv.at[1, k])

    for d in HOPS:
        yd, xd = lax.rem(y + d, 4), lax.rem(x + d, 4)

        @pl.when(order(yd, x) < EXTRA)
        def _(d=d, yd=yd):
            remote(re1.at[yd, :, :, last], e_all.at[y, :, :, last], s2x_send.at[0, d], s2x_recv.at[0], at(dy=d))

        @pl.when(order(y, xd) < EXTRA)
        def _(d=d, xd=xd):
            remote(rc1.at[xd, :, :, last], c_all.at[:, x, :, last], s2x_send.at[1, d], s2x_recv.at[1], at(dx=d))

    mine = order(y, x) < EXTRA

    @pl.when(mine)
    def _():
        local(re1.at[y, :, :, last], e_all.at[y, :, :, last], s2x_recv.at[0])
        local(rc1.at[x, :, :, last], c_all.at[:, x, :, last], s2x_recv.at[1])

    def gram(lo):
        @pl.loop(0, 4)
        def _(r):
            rows = pl.ds(pl.multiple_of(r * CH, CH), CH)
            left_e = e_all[r, :, :, lo : lo + 256].reshape(256, 256)
            left_c = c_all[r, :, :, lo : lo + 256].reshape(256, 256)
            for q in range(4):
                right = e_all[q, :, :, lo : lo + 256].reshape(256, 256)
                cols = slice(256 * q, 256 * q + 256)
                s = nt(left_e, right).reshape(CH, CH, 256) * consts[0][None]
                sacc[rows, cols] += jnp.sum(s, axis=1)
                p = nt(left_c, right).reshape(CH, CH, 256) * consts[2][None]
                pacc[rows, cols] += jnp.sum(p, axis=1)

    for j, (lo, width) in enumerate(CHUNKS):
        part = pl.ds(lo, width)
        await_bytes(e_all.at[:, :, :, part], s2_recv.at[0, j])
        await_bytes(c_all.at[:, :, :, part], s2_recv.at[1, j])
        if j == len(CHUNKS) - 1:

            @pl.when(mine)
            def _():
                await_bytes(e_all.at[:, :, :, last], s2x_recv.at[0])
                await_bytes(c_all.at[:, :, :, last], s2x_recv.at[1])

        gram(lo)

    group = lax.broadcasted_iota(jnp.int32, (ALL, 2 * MEMBERS), 0) // CH
    column = lax.broadcasted_iota(jnp.int32, (ALL, 2 * MEMBERS), 1)
    fold_s = (group == column).astype(F32)
    fold_p = (group == column - MEMBERS).astype(F32)
    sfull[...] = jnp.dot(sacc[...], fold_s, precision=HIGH, preferred_element_type=F32) + jnp.dot(
        pacc[...], fold_p, precision=HIGH, preferred_element_type=F32
    )
    half = MEMBERS // 2
    own = pl.ds(pl.multiple_of(half * c, half), half)
    other = pl.ds(pl.multiple_of(half * (1 - c), half), half)

    def swap(src, dst, sem, device):
        return pltpu.make_async_remote_copy(
            src_ref=src,
            dst_ref=dst,
            send_sem=sem.at[0],
            recv_sem=sem.at[1],
            device_id=device,
            device_id_type=MESH,
        )

    copy = swap(sfull.at[other], cbuf, c_sem, at(dc=1))
    copy.start()
    copy.wait()
    ysrc[...] = sfull[own] + cbuf[...]
    for src, buf, sem, nxt, where in (
        (ysrc, ybuf, y_sem, xsrc, [at(dy=d) for d in (1, 2, 3)]),
        (xsrc, xbuf, x_sem, zsrc, [at(dx=d) for d in (1, 2, 3)]),
        (zsrc, zbuf, z_sem, sfin, [at(dz=d) for d in range(1, NZ)]),
    ):
        copies = [swap(src, buf.at[i], sem.at[i], device) for i, device in enumerate(where)]
        for copy in copies:
            copy.start()
        for copy in copies:
            copy.wait()
        total = src[...]
        for i in range(len(where)):
            total += buf[i]
        if nxt is sfin:
            sfin[own] = total
        else:
            nxt[...] = total
    copy = swap(sfin.at[own], sfin.at[own], f_sem, at(dc=1))
    copy.start()
    copy.wait()

    scores = scale * sfin[:, :MEMBERS]
    pairs = sfin[:, MEMBERS:]
    peak = jnp.max(scores, axis=1, keepdims=True)
    exponent = jnp.exp(scores - peak)
    weights = exponent / jnp.sum(exponent, axis=1, keepdims=True)
    grad_scores = weights * (pairs - jnp.sum(weights * pairs, axis=1, keepdims=True))
    w_half = weights.astype(BF16)
    g_half = (scale * grad_scores).astype(BF16)
    spread = (
        lax.broadcasted_iota(jnp.int32, (MEMBERS, ALL), 0)
        == lax.broadcasted_iota(jnp.int32, (MEMBERS, ALL), 1) // CH
    ).astype(BF16)
    wexp[...] = jnp.dot(w_half, spread, preferred_element_type=F32)
    gexp[...] = jnp.dot(g_half, spread, preferred_element_type=F32)
    wtexp[...] = tn(w_half, spread)
    gtexp[...] = tn(g_half, spread)

    def times(coefficients, row, const):
        line = jnp.broadcast_to(coefficients[pl.ds(row, 1), :], (CH, ALL))
        return line * jnp.concatenate([consts[const]] * 4, axis=1)

    @pl.loop(0, 4)
    def _(i):
        d = hop(i)
        yh, xh = lax.rem(y + d, 4), lax.rem(x + d, 4)

        @pl.loop(0, CH)
        def _(k):
            rows = pl.ds(pl.multiple_of(k * CH, CH), CH)
            dblk[rows, :] = times(wexp, yh * CH + k, 2).astype(BF16)

        for q in range(3):
            part = slice(256 * q, 256 * q + 256)
            right = e_all[:, :, :, part].reshape(ALL, 256)
            out = jnp.dot(dblk[...], right, preferred_element_type=F32)
            bm[yh, :, :, part] = out.astype(BF16).reshape(4, ROWS, 256)

        main = pl.ds(0, XLO)

        @pl.when(i < 3)
        def _():
            remote(
                bm.at[yh, :, :, main], rb.at[y, :, :, main], q1_send.at[0], q1_recv.at[0, y], (yh, x, z, c)
            )

            @pl.when(mine)
            def _():
                remote(
                    bm.at[yh, :, :, last], rb.at[y, :, :, last], q1x_send.at[0], q1x_recv.at[0, y], (yh, x, z, c)
                )

        @pl.when(i == 3)
        def _():
            local(bm.at[yh, :, :, main], rb.at[y, :, :, main], q1_recv.at[0, y])

            @pl.when(mine)
            def _():
                local(bm.at[yh, :, :, last], rb.at[y, :, :, last], q1x_recv.at[0, y])

        @pl.loop(0, CH)
        def _(k):
            rows = pl.ds(pl.multiple_of(k * CH, CH), CH)
            row = (k // 4) * CH + xh * 4 + lax.rem(k, 4)
            tblk[rows, :] = times(wtexp, row, 3).astype(BF16)
            gblk[rows, :] = (times(gexp, row, 0) + times(gtexp, row, 1)).astype(BF16)

        for q in range(3):
            part = slice(256 * q, 256 * q + 256)
            right = e_all[:, :, :, part].reshape(ALL, 256)
            out = jnp.dot(gblk[...], right, preferred_element_type=F32)
            right = c_all[:, :, :, part].reshape(ALL, 256)
            out += jnp.dot(tblk[...], right, preferred_element_type=F32)
            gm[xh, :, :, part] = out.astype(BF16).reshape(4, ROWS, 256)

        @pl.when(i < 3)
        def _():
            remote(
                gm.at[xh, :, :, main], rg.at[x, :, :, main], q1_send.at[1], q1_recv.at[1, x], (y, xh, z, c)
            )

            @pl.when(mine)
            def _():
                remote(
                    gm.at[xh, :, :, last], rg.at[x, :, :, last], q1x_send.at[1], q1x_recv.at[1, x], (y, xh, z, c)
                )

        @pl.when(i == 3)
        def _():
            local(gm.at[xh, :, :, main], rg.at[x, :, :, main], q1_recv.at[1, x])

            @pl.when(mine)
            def _():
                local(gm.at[xh, :, :, last], rg.at[x, :, :, last], q1x_recv.at[1, x])

    @pl.loop(0, 4)
    def _(i):
        s = lax.rem(8 - hop(i), 4)
        ys, xs = lax.rem(y + s, 4), lax.rem(x + s, 4)
        main = pl.ds(0, XLO)
        await_bytes(rb.at[ys, :, :, main], q1_recv.at[0, ys])
        await_bytes(rg.at[xs, :, :, main], q1_recv.at[1, xs])
        for d in HOPS:
            xh, yh = lax.rem(x + d, 4), lax.rem(y + d, 4)
            remote(
                rb.at[ys, xh, :, main], ob.at[:, lanes(ys, x, 0, XLO)], q2_send.at[0], o_recv.at[0], at(dx=d)
            )
            remote(
                rg.at[xs, yh, :, main], og.at[:, lanes(y, xs, 0, XLO)], q2_send.at[1], o_recv.at[1], at(dy=d)
            )
        local(rb.at[ys, x, :, main], ob.at[:, lanes(ys, x, 0, XLO)], o_recv.at[0])
        local(rg.at[xs, y, :, main], og.at[:, lanes(y, xs, 0, XLO)], o_recv.at[1])

        @pl.when(order(ys, x) < EXTRA)
        def _():
            await_bytes(rb.at[ys, :, :, last], q1x_recv.at[0, ys])
            for d in HOPS:
                xh = lax.rem(x + d, 4)
                remote(
                    rb.at[ys, xh, :, last], ob.at[:, extra_lanes(ys, x)], q2x_send.at[0, ys], o_recv.at[0], at(dx=d)
                )
            local(rb.at[ys, x, :, last], ob.at[:, extra_lanes(ys, x)], o_recv.at[0])

        @pl.when(order(y, xs) < EXTRA)
        def _():
            await_bytes(rg.at[xs, :, :, last], q1x_recv.at[1, xs])
            for d in HOPS:
                yh = lax.rem(y + d, 4)
                remote(
                    rg.at[xs, yh, :, last], og.at[:, extra_lanes(y, xs)], q2x_send.at[1, xs], o_recv.at[1], at(dy=d)
                )
            local(rg.at[xs, y, :, last], og.at[:, extra_lanes(y, xs)], o_recv.at[1])

    for t in range(2):
        buf = (re1, rc1)[t]
        await_bytes(buf.at[pl.ds(0, 3), :, :, pl.ds(0, XLO)], s1_send.at[t])
        await_bytes(buf.at[pl.ds(0, 3), :, :, pl.ds(0, XLO)], s2_send.at[t])
        await_bytes(buf.at[pl.ds(0, 3), :, :, pl.ds(0, XLO)], q1_send.at[t])
        await_bytes(buf.at[pl.ds(0, 3), :, :, pl.ds(0, XLO)], q2_send.at[t])

        @pl.when(mine)
        def _(t=t, buf=buf):
            await_bytes(buf.at[pl.ds(0, 3), :, :, last], q1x_send.at[t])

    for d in HOPS:
        xd, yd = lax.rem(x + d, 4), lax.rem(y + d, 4)
        for k in range(4):

            @pl.when(order(k, xd) < EXTRA)
            def _(d=d, k=k):
                await_bytes(re1.at[k, 0, :, last], s1x_send.at[0, d, k])

            @pl.when(order(yd, k) < EXTRA)
            def _(d=d, k=k):
                await_bytes(rc1.at[k, 0, :, last], s1x_send.at[1, d, k])

        @pl.when(order(yd, x) < EXTRA)
        def _(d=d):
            await_bytes(re1.at[0, :, :, last], s2x_send.at[0, d])

        @pl.when(order(y, xd) < EXTRA)
        def _(d=d):
            await_bytes(rc1.at[0, :, :, last], s2x_send.at[1, d])

    for k in range(4):

        @pl.when(order(k, x) < EXTRA)
        def _(k=k):
            await_bytes(re1.at[0, pl.ds(0, 3), :, last], q2x_send.at[0, k])

        @pl.when(order(y, k) < EXTRA)
        def _(k=k):
            await_bytes(rc1.at[0, pl.ds(0, 3), :, last], q2x_send.at[1, k])

    await_bytes(ob, o_recv.at[0])
    await_bytes(og, o_recv.at[1])


def shards(scale, ensemble, cotangent, w_query, w_key, w_value, w_out):
    shape = ensemble.shape
    field = lambda: pltpu.VMEM((4, 4, ROWS, WIDTH), BF16)
    small = lambda *lead: pltpu.VMEM(lead + (MEMBERS // 2, 2 * MEMBERS), F32)
    dma = pltpu.SemaphoreType.DMA
    flat = jax.ShapeDtypeStruct((ROWS, CELL_DEV), BF16)
    hbm = pl.BlockSpec(memory_space=pl.ANY)
    vmem = pl.BlockSpec(memory_space=pltpu.VMEM)
    branch, grad = pl.pallas_call(
        functools.partial(kernel, scale),
        out_shape=(flat, flat),
        in_specs=[hbm, hbm, vmem, vmem, vmem, vmem],
        out_specs=(hbm, hbm),
        scratch_shapes=[field() for _ in range(8)]
        + [
            pltpu.VMEM((MEMBERS, ALL), F32),
            pltpu.VMEM((MEMBERS, ALL), F32),
            pltpu.VMEM((4, CH, 256), F32),
            pltpu.VMEM((MEMBERS, 2 * MEMBERS), F32),
            small(),
            small(),
            small(3),
            small(),
            small(3),
            small(),
            small(NZ - 1),
            pltpu.VMEM((MEMBERS, 2 * MEMBERS), F32),
        ]
        + [pltpu.VMEM((MEMBERS, ALL), F32) for _ in range(4)]
        + [pltpu.VMEM((256, ALL), BF16) for _ in range(3)]
        + [
            dma((2,)),
            dma((2, 3)),
            dma((2, 4, 4)),
            dma((2, 4)),
            dma((2,)),
            dma((2, 3)),
            dma((2, 4)),
            dma((2,)),
            dma((2,)),
            dma((3, 2)),
            dma((3, 2)),
            dma((NZ - 1, 2)),
            dma((2,)),
            dma((2,)),
            dma((2, 4)),
            dma((2,)),
            dma((2, 4)),
            dma((2,)),
            dma((2, 4)),
            dma((2,)),
        ],
        compiler_params=pltpu.CompilerParams(
            collective_id=0, has_side_effects=True, vmem_limit_bytes=48 * 2**20
        ),
    )(
        ensemble.reshape(ROWS, CELL_DEV),
        cotangent.reshape(ROWS, CELL_DEV),
        w_query,
        w_key,
        w_value,
        w_out,
    )
    updated = ensemble.astype(F32) + branch.reshape(shape).astype(F32)
    ensemble_grad = cotangent.astype(F32) + grad.reshape(shape).astype(F32)
    return updated, ensemble_grad


def solution(mesh):
    torus = Mesh(mesh.devices.reshape(NY, NX, NZ, NC), ("y", "x", "z", "c"))
    scale = 1.0 / (CELL_DEV * NZ * NC * math.sqrt(CH))
    placed = P(("y", "x"), None, ("z", "c"))
    return jax.shard_map(
        functools.partial(shards, scale),
        mesh=torus,
        in_specs=(placed, placed, P(), P(), P(), P()),
        out_specs=(placed, placed),
        check_vma=False,
    )
```

time: 288 us -> 110 us (0.38)
  blocking collectives: 156 us -> 0 us
  Pallas kernels: 0 us -> 101 us
  local copies, waits for them, and re-layouts: 99.6 us -> 5.48 us
  matrix products: 20.4 us -> 0 us
  other arithmetic: 8.86 us -> 3.14 us
    pallas_call x0 -> x1, Pallas kernels: none -> 101 us  [shards(): pl.pallas_call(functools.partial(kernel, scale), out_shape=(flat, flat),...]
    all_to_all x2 -> x0, blocking collectives: 86.4 us -> none  [side_by_side(): lax.all_to_all(both, axis, split_axis=split_dim, concat_axis=concat_dim,...]
    psum x4 -> x0, blocking collectives: 70.1 us -> none  [over_axes(): return functools.reduce(lax.psum, axes, value)]
    reshape x8 -> x0, local copies, waits for them, and re-layouts: 33 us -> none  [the longest x4 17.7 us: combine(): return mixed.astype(jnp.bfloat16).reshape(field.shape)]
    unnamed x28 -> x12, local copies, waits for them, and re-layouts: 32.8 us -> 5.48 us
    all_to_all x3 -> x0, local copies, waits for them, and re-layouts: 22.8 us -> none  [side_by_side(): lax.all_to_all(both, axis, split_axis=split_dim, concat_axis=concat_dim,...]
    dot_general x14 -> x0, matrix products: 20.4 us -> none  [the longest x4 5.92 us: combine(): jnp.dot(weights_half, flatten(field), preferred_element_type=jnp.float32)]
    concatenate x1 -> x0, local copies, waits for them, and re-layouts: 10.9 us -> none  [side_by_side(): both = jnp.concatenate(arrays, axis=along)]
where the time goes in v1:
time: 110 us
  Pallas kernels  101 us (92%)
  local copies, waits for them, and re-layouts  5.48 us (5%)
  other arithmetic  3.14 us (3%)
    pallas_call x1, Pallas kernels, shards(): pl.pallas_call(functools.partial(kernel, scale), out_shape=(flat, flat),...  101 us
    unnamed x12, local copies, waits for them, and re-layouts  5.48 us
    add x1, other arithmetic, shards(): ensemble_grad = cotangent.astype(F32) + grad.reshape(shape).astype(F32)  3.14 us

profile of v1, /device:TPU:1, one launch (start us, length us, event | category | flops | bytes accessed | tf_op | source)
XLA Modules:
  0.0 110.0 jit_solution(6360492871240625439)
XLA Ops:
  0.6 0.0 copy-start
  0.6 1.4 %copy-done = bf16[4,16,11520]{2,1,0:T(8,128)(2,1)S(1)} copy-done((bf16[4,16,11520]{2,1,0:T(8,128)(2,1)S(1)}, bf16[4,16,11520]{2,1,0:T(8,128)(2,1)}, u32[]{:S(2)}) %copy-start) | copy-done | bytes 1474584
  2.0 0.0 copy-start.1
  2.0 1.4 %copy-done.1 = bf16[4,16,11520]{2,1,0:T(8,128)(2,1)S(1)} copy-done((bf16[4,16,11520]{2,1,0:T(8,128)(2,1)S(1)}, bf16[4,16,11520]{2,1,0:T(8,128)(2,1)}, u32[]{:S(2)}) %copy-start.1) | copy-done | bytes 1474584
  3.4 0.0 copy-start.2
  3.4 0.7 copy-done.2
  4.1 0.0 copy-start.3
  4.1 0.7 copy-done.3
  4.8 0.0 copy-start.4
  4.8 0.7 copy-done.4
  5.4 0.0 copy-start.5
  5.4 0.7 copy-done.5
  6.1 100.7 %shard_map.77 = (bf16[64,11520]{1,0:T(8,128)(2,1)S(1)}, bf16[64,11520]{1,0:T(8,128)(2,1)S(1)}) custom-call(bf16[64,11520]{1,0:T(8,128)(2,1)S(1)} %bitcast.6, bf16[64,11520]{1,0:T(8,128)(2,1)S(1)} %bitcast.7, bf16[16,16]{1,0:T(8,128)(2,1)S(1)} %copy-done.2, bf16[16,16]{1,0:T(8,128)(2,1)S(1)} %copy-done.3, bf16[16,16]{1,0:T(8,128)(2,1)S(1)} %copy-done.4, ...), custom_call_target="tpu_custom_call" | custom-call | tf_op jit(solution)/shard_map/pallas_call | solution.py:528
  106.8 3.1 %convert_add_fusion = (f32[4,16,11520]{2,1,0:T(8,128)}, f32[4,16,11520]{2,1,0:T(8,128)}) fusion(bf16[4,16,11520]{2,1,0:T(8,128)(2,1)S(1)} %bitcast.9, bf16[4,16,11520]{2,1,0:T(8,128)(2,1)S(1)} %copy-done.1, bf16[4,16,11520]{2,1,0:T(8,128)(2,1)S(1)} %bitcast.8, bf16[4,16,11520]{2,1,0:T(8,128)(2,1)S(1)} %copy-done), kind=kLoop, calls=%fused_computation | loop fusion | flops 4423680 | bytes 11796480 | tf_op jit(solution)/shard_map/add | solution.py:584
Async XLA Ops:
  0.6 1.4 %copy-start = (bf16[4,16,11520]{2,1,0:T(8,128)(2,1)S(1)}, bf16[4,16,11520]{2,1,0:T(8,128)(2,1)}, u32[]{:S(2)}) copy-start(bf16[4,16,11520]{2,1,0:T(8,128)(2,1)} %param.6) | copy-start | bytes 4423684
  2.0 1.4 %copy-start.1 = (bf16[4,16,11520]{2,1,0:T(8,128)(2,1)S(1)}, bf16[4,16,11520]{2,1,0:T(8,128)(2,1)}, u32[]{:S(2)}) copy-start(bf16[4,16,11520]{2,1,0:T(8,128)(2,1)} %param.7) | copy-start | bytes 4423684
  3.4 0.7 copy-start.2
  4.1 0.7 copy-start.3
  4.8 0.7 copy-start.4
  5.4 0.7 copy-start.5

commit v2 on v0

v2 whole, which is shorter than its diff:
```python
import functools
import math

import jax
import jax.numpy as jnp
from jax import lax
from jax.experimental import pallas as pl
from jax.experimental.pallas import tpu as pltpu
from jax.sharding import Mesh
from jax.sharding import PartitionSpec as P

MESH = pl.DeviceIdType.MESH
F32 = jnp.float32
BF16 = jnp.bfloat16
HIGH = lax.Precision.HIGHEST

NX, NY, NZ, NC = 4, 4, 8, 2
PEERS = NX * NY
CH = 16
MEM_DEV = 4
ROWS = MEM_DEV * CH
MEMBERS = MEM_DEV * PEERS
ALL = ROWS * PEERS
TILE = 128
MAIN = 5
EXTRA = 10
WIDTH = (MAIN + 1) * TILE
CELL_DEV = 11520
SPAN = 3 * TILE
XLO = MAIN * TILE
HOPS = (1, 3, 2)


def nt(a, b, precision=None):
    return lax.dot_general(
        a, b, (((1,), (1,)), ((), ())), precision=precision, preferred_element_type=F32
    )


def tn(a, b, precision=None):
    return lax.dot_general(
        a, b, (((0,), (0,)), ((), ())), precision=precision, preferred_element_type=F32
    )


def kernel(
    scale,
    e_hbm,
    c_hbm,
    wq_hbm,
    wk_hbm,
    wv_hbm,
    wo_hbm,
    ob,
    og,
    weights_in,
    ea1,
    eb1,
    ca1,
    cb1,
    e_all,
    c_all,
    bm,
    gm,
    ba,
    bb,
    ga,
    gb,
    partial,
    dmat,
    tmat,
    gmat,
    acc,
    consts,
    fold_lo,
    fold_hi,
    packed,
    cbuf,
    ysrc,
    ybuf,
    xsrc,
    xbuf,
    zsrc,
    zbuf,
    fin,
    wsave,
    exp_a,
    exp_b,
    w_sem,
    s1_send,
    s1_recv,
    s1x_send,
    s1x_recv,
    s2_send,
    s2_recv,
    s2x_send,
    s2x_recv,
    c_sem,
    y_sem,
    x_sem,
    z_sem,
    f_sem,
    q1_send,
    q1_recv,
    q1x_send,
    q1x_recv,
    q2_send,
    q2x_send,
    o_recv,
):
    y, x = lax.axis_index("y"), lax.axis_index("x")
    z, c = lax.axis_index("z"), lax.axis_index("c")
    sources = (e_hbm, c_hbm)
    first_a, first_b = (ea1, ca1), (eb1, cb1)
    whole = (e_all, c_all)
    made = (bm, gm)
    back_a, back_b = (ba, ga), (bb, gb)
    homes = (ob, og)

    def at(dy=0, dx=0, dz=0, dc=0):
        return (
            lax.rem(y + dy, NY),
            lax.rem(x + dx, NX),
            lax.rem(z + dz, NZ),
            lax.rem(c + dc, NC),
        )

    def more(yd, xd):
        return 4 * lax.rem(xd + yd + 2 * c, 4) + yd

    def has_more(yd, xd):
        return more(yd, xd) < EXTRA

    def lanes(yd, xd, lo):
        return pl.ds(pl.multiple_of((4 * yd + xd) * XLO + lo, TILE), TILE)

    def more_lanes(yd, xd):
        return pl.ds(pl.multiple_of((MAIN * PEERS + more(yd, xd)) * TILE, TILE), TILE)

    def remote(src, dst, send, recv, device):
        pltpu.make_async_remote_copy(
            src_ref=src, dst_ref=dst, send_sem=send, recv_sem=recv, device_id=device, device_id_type=MESH
        ).start()

    def local(src, dst, sem):
        pltpu.make_async_copy(src, dst, sem).start()

    def await_bytes(view, sem):
        pltpu.make_async_copy(view, view, sem).wait()

    mine = has_more(y, x)
    tile = [pl.ds(TILE * k, TILE) for k in range(6)]

    def out1(t, j):
        src, pa, pb = sources[t], first_a[t], first_b[t]
        for d in HOPS:

            @pl.loop(0, 4)
            def _(k, d=d):
                xd, yd = lax.rem(x + d, 4), lax.rem(y + d, 4)
                remote(
                    src.at[:, lanes(k, xd, TILE * j)],
                    pa.at[k, x, :, tile[j]],
                    s1_send.at[t, 0],
                    s1_recv.at[t, 0, j],
                    at(dx=d),
                )
                if j < 2:
                    remote(
                        src.at[:, lanes(yd, k, SPAN + TILE * j)],
                        pb.at[k, y, :, tile[j]],
                        s1_send.at[t, 1],
                        s1_recv.at[t, 1, j],
                        at(dy=d),
                    )
                else:

                    @pl.when(has_more(yd, k))
                    def _():
                        remote(
                            src.at[:, more_lanes(yd, k)],
                            pb.at[k, y, :, tile[j]],
                            s1x_send.at[t, d, k],
                            s1x_recv.at[t, k],
                            at(dy=d),
                        )

        @pl.loop(0, 4)
        def _(k):
            local(src.at[:, lanes(k, x, TILE * j)], pa.at[k, x, :, tile[j]], s1_recv.at[t, 0, j])
            if j < 2:
                local(src.at[:, lanes(y, k, SPAN + TILE * j)], pb.at[k, y, :, tile[j]], s1_recv.at[t, 1, j])
            else:

                @pl.when(has_more(y, k))
                def _():
                    local(src.at[:, more_lanes(y, k)], pb.at[k, y, :, tile[j]], s1x_recv.at[t, k])

    def out2(t, j):
        pa, pb, dst = first_a[t], first_b[t], whole[t]
        await_bytes(pa.at[:, :, :, tile[j]], s1_recv.at[t, 0, j])
        for d in HOPS:
            yd = lax.rem(y + d, 4)
            remote(
                pa.at[yd, :, :, tile[j]], dst.at[y, :, :, tile[j]], s2_send.at[t, 0], s2_recv.at[t, 0, j], at(dy=d)
            )
        local(pa.at[y, :, :, tile[j]], dst.at[y, :, :, tile[j]], s2_recv.at[t, 0, j])
        if j < 2:
            await_bytes(pb.at[:, :, :, tile[j]], s1_recv.at[t, 1, j])
            for d in HOPS:
                xd = lax.rem(x + d, 4)
                remote(
                    pb.at[xd, :, :, tile[j]],
                    dst.at[:, x, :, tile[3 + j]],
                    s2_send.at[t, 1],
                    s2_recv.at[t, 1, j],
                    at(dx=d),
                )
            local(pb.at[x, :, :, tile[j]], dst.at[:, x, :, tile[3 + j]], s2_recv.at[t, 1, j])
        else:
            for d in HOPS:
                xd = lax.rem(x + d, 4)

                @pl.when(has_more(y, xd))
                def _(d=d, xd=xd):
                    await_bytes(pb.at[xd, :, :, tile[j]], s1x_recv.at[t, xd])
                    remote(
                        pb.at[xd, :, :, tile[j]],
                        dst.at[:, x, :, tile[3 + j]],
                        s2x_send.at[t, d],
                        s2x_recv.at[t],
                        at(dx=d),
                    )

            @pl.when(mine)
            def _():
                await_bytes(pb.at[x, :, :, tile[j]], s1x_recv.at[t, x])
                local(pb.at[x, :, :, tile[j]], dst.at[:, x, :, tile[3 + j]], s2x_recv.at[t])

    def arrived(t, j):
        await_bytes(whole[t].at[:, :, :, tile[j]], s2_recv.at[t, 0, j])
        if j < 2:
            await_bytes(whole[t].at[:, :, :, tile[3 + j]], s2_recv.at[t, 1, j])
        else:

            @pl.when(mine)
            def _():
                await_bytes(whole[t].at[:, :, :, tile[3 + j]], s2x_recv.at[t])

    def home1(t, j):
        src, pa, pb = made[t], back_a[t], back_b[t]
        for d in HOPS:
            yh, xh = lax.rem(y + d, 4), lax.rem(x + d, 4)
            remote(
                src.at[yh, :, :, tile[j]], pa.at[y, :, :, tile[j]], q1_send.at[t, 0], q1_recv.at[t, 0, j], at(dy=d)
            )
            if j < 2:
                remote(
                    src.at[:, xh, :, tile[3 + j]],
                    pb.at[x, :, :, tile[j]],
                    q1_send.at[t, 1],
                    q1_recv.at[t, 1, j],
                    at(dx=d),
                )
        local(src.at[y, :, :, tile[j]], pa.at[y, :, :, tile[j]], q1_recv.at[t, 0, j])
        if j < 2:
            local(src.at[:, x, :, tile[3 + j]], pb.at[x, :, :, tile[j]], q1_recv.at[t, 1, j])
        else:

            @pl.when(mine)
            def _():
                for d in HOPS:
                    xh = lax.rem(x + d, 4)
                    remote(
                        src.at[:, xh, :, tile[3 + j]],
                        pb.at[x, :, :, tile[j]],
                        q1x_send.at[t],
                        q1x_recv.at[t, x],
                        at(dx=d),
                    )
                local(src.at[:, x, :, tile[3 + j]], pb.at[x, :, :, tile[j]], q1x_recv.at[t, x])

    def home2(t, j):
        pa, pb, dst = back_a[t], back_b[t], homes[t]
        await_bytes(pa.at[:, :, :, tile[j]], q1_recv.at[t, 0, j])

        @pl.loop(0, 4)
        def _(s):
            for d in HOPS:
                remote(
                    pa.at[s, lax.rem(x + d, 4), :, tile[j]],
                    dst.at[:, lanes(s, x, TILE * j)],
                    q2_send.at[t, 0],
                    o_recv.at[t],
                    at(dx=d),
                )
            local(pa.at[s, x, :, tile[j]], dst.at[:, lanes(s, x, TILE * j)], o_recv.at[t])

        if j < 2:
            await_bytes(pb.at[:, :, :, tile[j]], q1_recv.at[t, 1, j])

        @pl.loop(0, 4)
        def _(s):
            if j < 2:
                for d in HOPS:
                    remote(
                        pb.at[s, lax.rem(y + d, 4), :, tile[j]],
                        dst.at[:, lanes(y, s, SPAN + TILE * j)],
                        q2_send.at[t, 1],
                        o_recv.at[t],
                        at(dy=d),
                    )
                local(pb.at[s, y, :, tile[j]], dst.at[:, lanes(y, s, SPAN + TILE * j)], o_recv.at[t])
            else:

                @pl.when(has_more(y, s))
                def _():
                    await_bytes(pb.at[s, :, :, tile[j]], q1x_recv.at[t, s])
                    for d in HOPS:
                        remote(
                            pb.at[s, lax.rem(y + d, 4), :, tile[j]],
                            dst.at[:, more_lanes(y, s)],
                            q2x_send.at[t, s],
                            o_recv.at[t],
                            at(dy=d),
                        )
                    local(pb.at[s, y, :, tile[j]], dst.at[:, more_lanes(y, s)], o_recv.at[t])

    def cells(t, j, r=None):
        ref = whole[t]
        if r is None:
            two = [ref[:, :, :, tile[k]].reshape(ALL, TILE) for k in (j, 3 + j)]
        else:
            two = [ref[r, :, :, tile[k]].reshape(256, TILE) for k in (j, 3 + j)]
        return jnp.concatenate(two, axis=1)

    def gram(t, j, const):
        @pl.loop(0, 4)
        def _(r):
            rows = pl.ds(pl.multiple_of(r * CH, CH), CH)
            left = cells(t, j, r)
            for q in range(4):
                cols = slice(256 * q, 256 * q + 256)
                s = nt(left, cells(0, j, q)).reshape(CH, CH, 256) * consts[const][None]
                if j == 0:
                    acc[rows, cols] = jnp.sum(s, axis=1)
                else:
                    acc[rows, cols] += jnp.sum(s, axis=1)

    half = MEMBERS // 4
    own = pl.ds(pl.multiple_of(half * c, half), half)
    other = pl.ds(pl.multiple_of(half * (1 - c), half), half)

    def pack(t):
        rest = acc[...]
        total = None
        for _ in range(3):
            part = rest.astype(BF16)
            rest = rest - part.astype(F32)
            both = jnp.dot(part[: MEMBERS // 2], fold_lo[...], preferred_element_type=F32)
            both += jnp.dot(part[MEMBERS // 2 :], fold_hi[...], preferred_element_type=F32)
            total = both if total is None else total + both
        packed[t] = total

    def swap(src, dst, send, recv, device):
        return pltpu.make_async_remote_copy(
            src_ref=src, dst_ref=dst, send_sem=send, recv_sem=recv, device_id=device, device_id_type=MESH
        )

    def run(copies):
        for copy in copies:
            copy.start()

    def collect(t, copies, src, buf, dst):
        for copy in copies:
            copy.wait()
        total = src[t]
        for i in range(len(copies)):
            total += buf[t, i]
        if dst is fin:
            fin[t, own] = total
        else:
            dst[t] = total

    def stage(t, name):
        if name == "core":
            return [swap(packed.at[t, other], cbuf.at[t], c_sem.at[t, 0], c_sem.at[t, 1], at(dc=1))]
        if name == "back":
            return [swap(fin.at[t, own], fin.at[t, own], f_sem.at[t, 0], f_sem.at[t, 1], at(dc=1))]
        src, buf, sem, key, count = {
            "y": (ysrc, ybuf, y_sem, "dy", NY),
            "x": (xsrc, xbuf, x_sem, "dx", NX),
            "z": (zsrc, zbuf, z_sem, "dz", NZ),
        }[name]
        return [
            swap(src.at[t], buf.at[t, d - 1], sem.at[t, d - 1, 0], sem.at[t, d - 1, 1], at(**{key: d}))
            for d in range(1, count)
        ]

    def reduce_begin(t, between):
        pack(t)
        core = stage(t, "core")
        run(core)
        core[0].wait()
        ysrc[t] = packed[t, own] + cbuf[t]
        along = stage(t, "y")
        run(along)
        between(1)
        collect(t, along, ysrc, ybuf, xsrc)
        along = stage(t, "x")
        run(along)
        between(2)
        collect(t, along, xsrc, xbuf, zsrc)
        run(stage(t, "z"))

    def reduce_z(t):
        collect(t, stage(t, "z"), zsrc, zbuf, fin)
        run(stage(t, "back"))

    def reduce_end(t):
        stage(t, "back")[0].wait()
        return jnp.concatenate([fin[t, :, :MEMBERS], fin[t, :, MEMBERS:]], axis=0)

    spread = (
        lax.broadcasted_iota(jnp.int32, (MEMBERS, ALL), 0)
        == lax.broadcasted_iota(jnp.int32, (MEMBERS, ALL), 1) // CH
    ).astype(BF16)

    def blocks(dst, *terms):
        @pl.loop(0, MEMBERS)
        def _(m):
            rows = pl.ds(pl.multiple_of(m * CH, CH), CH)
            for q in range(4):
                cols = slice(256 * q, 256 * q + 256)
                total = None
                for coefficient, const in terms:
                    term = jnp.broadcast_to(coefficient[pl.ds(m, 1), cols], (CH, 256)) * consts[const]
                    total = term if total is None else total + term
                dst[rows, cols] = total.astype(BF16)

    def put(t, j, r, value):
        value = value.astype(BF16)
        made[t][r, :, :, tile[j]] = value[:, :TILE].reshape(4, ROWS, TILE)
        made[t][r, :, :, tile[3 + j]] = value[:, TILE:].reshape(4, ROWS, TILE)

    barrier = pltpu.get_barrier_semaphore()
    partners = [at(dc=1)]
    partners += [at(dy=d) for d in (1, 2, 3)] + [at(dx=d) for d in (1, 2, 3)]
    partners += [at(dz=d) for d in range(1, NZ)]
    for device in partners:
        pl.semaphore_signal(barrier, inc=1, device_id=device, device_id_type=MESH)
    for i, ref in enumerate((wq_hbm, wk_hbm, wv_hbm, wo_hbm)):
        local(ref, weights_in.at[i], w_sem)
    pl.semaphore_wait(barrier, len(partners))

    for j in range(3):
        out1(0, j)

    @pl.when(jnp.logical_not(mine))
    def _():
        e_all[:, :, :, XLO:] = jnp.zeros((4, 4, ROWS, TILE), BF16)
        c_all[:, :, :, XLO:] = jnp.zeros((4, 4, ROWS, TILE), BF16)

    await_bytes(weights_in, w_sem)
    wq, wk, wv, wo = (weights_in[i] for i in range(4))
    a_mat = tn(wq, wk)
    at_mat = tn(wk, wq)
    m_mat = jnp.dot(wo, wv, preferred_element_type=F32)
    mt_mat = lax.dot_general(wv, wo, (((0,), (1,)), ((), ())), preferred_element_type=F32)
    row16 = lax.broadcasted_iota(jnp.int32, (CH, 256), 0)
    lane16 = lax.rem(lax.broadcasted_iota(jnp.int32, (CH, 256), 1), CH)
    repeat = (row16 == lane16).astype(F32)
    for i, mat in enumerate((a_mat, at_mat, m_mat, mt_mat)):
        consts[i] = jnp.dot(mat, repeat, precision=HIGH, preferred_element_type=F32)
    group = lax.broadcasted_iota(jnp.int32, (ALL, 2 * MEMBERS), 0) // CH
    column = lax.broadcasted_iota(jnp.int32, (ALL, 2 * MEMBERS), 1)
    fold_lo[...] = (group == column).astype(BF16)
    fold_hi[...] = (group == column - MEMBERS).astype(BF16)

    for j in range(3):
        out2(0, j)
    out1(1, 0)
    for j in range(3):
        arrived(0, j)
        gram(0, j, 0)

    reduce_begin(0, lambda j: out1(1, j))
    out2(1, 0)
    out2(1, 1)
    reduce_z(0)
    out2(1, 2)
    scores = scale * reduce_end(0)
    exponent = jnp.exp(scores - jnp.max(scores, axis=1, keepdims=True))
    weights = exponent / jnp.sum(exponent, axis=1, keepdims=True)
    wsave[...] = weights
    w_half = weights.astype(BF16)
    exp_a[...] = jnp.dot(w_half, spread, preferred_element_type=F32)
    blocks(dmat, (exp_a, 2))

    def mix_branch(j):
        right = cells(0, j)
        for r in range(4):
            put(0, j, r, jnp.dot(dmat[256 * r : 256 * r + 256, :], right, preferred_element_type=F32))

    mix_branch(0)
    home1(0, 0)
    mix_branch(1)
    mix_branch(2)
    for j in range(3):
        arrived(1, j)
        gram(1, j, 2)

    reduce_begin(1, lambda j: home1(0, j))
    home2(0, 0)
    exp_b[...] = tn(wsave[...].astype(BF16), spread)
    blocks(tmat, (exp_b, 3))
    for j in range(3):
        right = cells(1, j)
        for r in range(4):
            rows = slice(256 * r, 256 * r + 256)
            partial[j, rows, :] = jnp.dot(tmat[rows, :], right, preferred_element_type=F32)
    home2(0, 1)
    reduce_z(1)
    home2(0, 2)
    pairs = reduce_end(1)
    weights = wsave[...]
    grad_scores = weights * (pairs - jnp.sum(weights * pairs, axis=1, keepdims=True))
    g_half = (scale * grad_scores).astype(BF16)
    exp_a[...] = jnp.dot(g_half, spread, preferred_element_type=F32)
    exp_b[...] = tn(g_half, spread)
    blocks(gmat, (exp_a, 0), (exp_b, 1))
    for j in range(3):
        right = cells(0, j)
        for r in range(4):
            rows = slice(256 * r, 256 * r + 256)
            out = jnp.dot(gmat[rows, :], right, preferred_element_type=F32)
            put(1, j, r, out + partial[j, rows, :])
        home1(1, j)
    for j in range(3):
        home2(1, j)

    for t in range(2):
        for sem in (s1_send, s2_send, q1_send, q2_send):
            await_bytes(ea1.at[pl.ds(0, 3)], sem.at[t, 0])
            await_bytes(ea1.at[pl.ds(0, 3), :, :, pl.ds(0, 2 * TILE)], sem.at[t, 1])

        @pl.when(mine)
        def _(t=t):
            await_bytes(ea1.at[pl.ds(0, 3), :, :, tile[2]], q1x_send.at[t])

        for d in HOPS:
            yd, xd = lax.rem(y + d, 4), lax.rem(x + d, 4)
            for k in range(4):

                @pl.when(has_more(yd, k))
                def _(t=t, d=d, k=k):
                    await_bytes(ea1.at[0, 0, :, tile[2]], s1x_send.at[t, d, k])

            @pl.when(has_more(y, xd))
            def _(t=t, d=d):
                await_bytes(ea1.at[0, :, :, tile[2]], s2x_send.at[t, d])

        for k in range(4):

            @pl.when(has_more(y, k))
            def _(t=t, k=k):
                await_bytes(ea1.at[0, pl.ds(0, 3), :, tile[2]], q2x_send.at[t, k])

        await_bytes(homes[t], o_recv.at[t])


def shards(scale, ensemble, cotangent, w_query, w_key, w_value, w_out):
    shape = ensemble.shape
    full = lambda: pltpu.VMEM((4, 4, ROWS, WIDTH), BF16)
    part = lambda: pltpu.VMEM((4, 4, ROWS, SPAN), BF16)
    square = lambda: pltpu.VMEM((ALL, ALL), BF16)
    small = lambda *lead: pltpu.VMEM((2,) + lead + (MEMBERS // 4, 2 * MEMBERS), F32)
    dma = pltpu.SemaphoreType.DMA
    flat = jax.ShapeDtypeStruct((ROWS, CELL_DEV), BF16)
    hbm = pl.BlockSpec(memory_space=pltpu.HBM)
    branch, grad = pl.pallas_call(
        functools.partial(kernel, scale),
        out_shape=(flat, flat),
        in_specs=[hbm] * 6,
        out_specs=(hbm, hbm),
        scratch_shapes=[pltpu.VMEM((4, CH, CH), BF16)]
        + [part() for _ in range(4)]
        + [full() for _ in range(4)]
        + [part() for _ in range(4)]
        + [pltpu.VMEM((3, ALL, 2 * TILE), F32)]
        + [square() for _ in range(3)]
        + [
            pltpu.VMEM((MEMBERS, ALL), F32),
            pltpu.VMEM((4, CH, 256), F32),
            pltpu.VMEM((ALL, 2 * MEMBERS), BF16),
            pltpu.VMEM((ALL, 2 * MEMBERS), BF16),
            pltpu.VMEM((2, MEMBERS // 2, 2 * MEMBERS), F32),
            small(),
            small(),
            small(3),
            small(),
            small(3),
            small(),
            small(NZ - 1),
            pltpu.VMEM((2, MEMBERS // 2, 2 * MEMBERS), F32),
            pltpu.VMEM((MEMBERS, MEMBERS), F32),
            pltpu.VMEM((MEMBERS, ALL), F32),
            pltpu.VMEM((MEMBERS, ALL), F32),
        ]
        + [
            dma,
            dma((2, 2)),
            dma((2, 2, 3)),
            dma((2, 4, 4)),
            dma((2, 4)),
            dma((2, 2)),
            dma((2, 2, 3)),
            dma((2, 4)),
            dma((2,)),
            dma((2, 2)),
            dma((2, 3, 2)),
            dma((2, 3, 2)),
            dma((2, NZ - 1, 2)),
            dma((2, 2)),
            dma((2, 2)),
            dma((2, 2, 3)),
            dma((2,)),
            dma((2, 4)),
            dma((2, 2)),
            dma((2, 4)),
            dma((2,)),
        ],
        compiler_params=pltpu.CompilerParams(
            collective_id=0, has_side_effects=True, vmem_limit_bytes=67043328
        ),
    )(
        ensemble.reshape(ROWS, CELL_DEV),
        cotangent.reshape(ROWS, CELL_DEV),
        w_query,
        w_key,
        w_value,
        w_out,
    )
    updated = ensemble.astype(F32) + branch.reshape(shape).astype(F32)
    ensemble_grad = cotangent.astype(F32) + grad.reshape(shape).astype(F32)
    return updated, ensemble_grad


def solution(mesh):
    torus = Mesh(mesh.devices.reshape(NY, NX, NZ, NC), ("y", "x", "z", "c"))
    scale = 1.0 / (CELL_DEV * NZ * NC * math.sqrt(CH))
    placed = P(("y", "x"), None, ("z", "c"))
    return jax.shard_map(
        functools.partial(shards, scale),
        mesh=torus,
        in_specs=(placed, placed, P(), P(), P(), P()),
        out_specs=(placed, placed),
        check_vma=False,
    )
```

time: 288 us -> 98.8 us (0.34)
  blocking collectives: 156 us -> 0 us
  local copies, waits for them, and re-layouts: 99.6 us -> 0 us
  Pallas kernels: 0 us -> 92.2 us
  matrix products: 20.4 us -> 0 us
  other arithmetic: 8.86 us -> 5.85 us
    pallas_call x0 -> x1, Pallas kernels: none -> 92.2 us  [shards(): pl.pallas_call(functools.partial(kernel, scale), out_shape=(flat, flat),...]
    all_to_all x2 -> x0, blocking collectives: 86.4 us -> none  [side_by_side(): lax.all_to_all(both, axis, split_axis=split_dim, concat_axis=concat_dim,...]
    psum x4 -> x0, blocking collectives: 70.1 us -> none  [over_axes(): return functools.reduce(lax.psum, axes, value)]
    reshape x8 -> x0, local copies, waits for them, and re-layouts: 33 us -> none  [the longest x4 17.7 us: combine(): return mixed.astype(jnp.bfloat16).reshape(field.shape)]
    unnamed x28 -> x0, local copies, waits for them, and re-layouts: 32.8 us -> none
    all_to_all x3 -> x0, local copies, waits for them, and re-layouts: 22.8 us -> none  [side_by_side(): lax.all_to_all(both, axis, split_axis=split_dim, concat_axis=concat_dim,...]
    dot_general x14 -> x0, matrix products: 20.4 us -> none  [the longest x4 5.92 us: combine(): jnp.dot(weights_half, flatten(field), preferred_element_type=jnp.float32)]
    concatenate x1 -> x0, local copies, waits for them, and re-layouts: 10.9 us -> none  [side_by_side(): both = jnp.concatenate(arrays, axis=along)]
where the time goes in v2:
time: 98.8 us; the launch traced here: 98.7 us
  Pallas kernels  92.2 us (93%)
  other arithmetic  5.85 us (6%)
    pallas_call x1, Pallas kernels, shards(): pl.pallas_call(functools.partial(kernel, scale), out_shape=(flat, flat),...  92.2 us
    add x1, other arithmetic, shards(): ensemble_grad = cotangent.astype(F32) + grad.reshape(shape).astype(F32)  5.85 us

profile of v2, /device:TPU:1, one launch (start us, length us, event | category | flops | bytes accessed | tf_op | source)
XLA Modules:
  0.0 98.7 jit_solution(3681887215799121154)
XLA Ops:
  0.6 92.2 %shard_map.77 = (bf16[64,11520]{1,0:T(8,128)(2,1)}, bf16[64,11520]{1,0:T(8,128)(2,1)}) custom-call(bf16[64,11520]{1,0:T(8,128)(2,1)} %bitcast.6, bf16[64,11520]{1,0:T(8,128)(2,1)} %bitcast.7, bf16[16,16]{1,0:T(8,128)(2,1)} %wq_hbm.1, bf16[16,16]{1,0:T(8,128)(2,1)} %wk_hbm.1, bf16[16,16]{1,0:T(8,128)(2,1)} %wv_hbm.1, bf16[16,16]{1,0:T(8,128)(2,1)} %wo_hbm.1), custom_call_target="tpu_custom_call" | custom-call | tf_op jit(solution)/shard_map/pallas_call | solution.py:581
  92.9 5.9 %convert_add_fusion = (f32[4,16,11520]{2,1,0:T(8,128)}, f32[4,16,11520]{2,1,0:T(8,128)}) fusion(bf16[4,16,11520]{2,1,0:T(8,128)(2,1)} %bitcast.9, bf16[4,16,11520]{2,1,0:T(8,128)(2,1)} %param.7, bf16[4,16,11520]{2,1,0:T(8,128)(2,1)} %bitcast.8, bf16[4,16,11520]{2,1,0:T(8,128)(2,1)} %param.6), kind=kLoop, calls=%fused_computation | loop fusion | flops 4423680 | bytes 11796480 | tf_op jit(solution)/shard_map/add | solution.py:645

commit v3 on v2

--- a/solution.py
+++ b/solution.py
@@ -29,12 +29,8 @@
 SPAN = 3 * TILE
 XLO = MAIN * TILE
 HOPS = (1, 3, 2)
-
-
-def nt(a, b, precision=None):
-    return lax.dot_general(
-        a, b, (((1,), (1,)), ((), ())), precision=precision, preferred_element_type=F32
-    )
+PLANE = [(dy, dx) for dy in HOPS + (0,) for dx in HOPS + (0,) if dy or dx]
+PLANE.sort(key=lambda d: -(min(d[0], 4 - d[0]) + min(d[1], 4 - d[1])))
 
 
 def tn(a, b, precision=None):
@@ -53,6 +49,8 @@
     wo_hbm,
     ob,
     og,
+    e_out,
+    c_out,
     weights_in,
     ea1,
     eb1,
@@ -70,6 +68,7 @@
     dmat,
     tmat,
     gmat,
+    turned,
     acc,
     consts,
     fold_lo,
@@ -78,8 +77,6 @@
     cbuf,
     ysrc,
     ybuf,
-    xsrc,
-    xbuf,
     zsrc,
     zbuf,
     fin,
@@ -87,6 +84,7 @@
     exp_a,
     exp_b,
     w_sem,
+    k_sem,
     s1_send,
     s1_recv,
     s1x_send,
@@ -97,7 +95,6 @@
     s2x_recv,
     c_sem,
     y_sem,
-    x_sem,
     z_sem,
     f_sem,
     q1_send,
@@ -334,6 +331,10 @@
             two = [ref[r, :, :, tile[k]].reshape(256, TILE) for k in (j, 3 + j)]
         return jnp.concatenate(two, axis=1)
 
+    def turn(j):
+        for q in range(4):
+            turned[j, :, 256 * q : 256 * q + 256] = cells(0, j, q).T
+
     def gram(t, j, const):
         @pl.loop(0, 4)
         def _(r):
@@ -341,26 +342,30 @@
             left = cells(t, j, r)
             for q in range(4):
                 cols = slice(256 * q, 256 * q + 256)
-                s = nt(left, cells(0, j, q)).reshape(CH, CH, 256) * consts[const][None]
+                s = jnp.dot(left, turned[j, :, cols], preferred_element_type=F32)
+                s = s.reshape(CH, CH, 256) * consts[const][None]
+                s = jnp.sum(s, axis=1)
                 if j == 0:
-                    acc[rows, cols] = jnp.sum(s, axis=1)
+                    acc[t, rows, cols] = s
                 else:
-                    acc[rows, cols] += jnp.sum(s, axis=1)
+                    acc[t, rows, cols] += s
 
     half = MEMBERS // 4
     own = pl.ds(pl.multiple_of(half * c, half), half)
     other = pl.ds(pl.multiple_of(half * (1 - c), half), half)
 
     def pack(t):
-        rest = acc[...]
-        total = None
+        rest = acc[t]
+        parts = []
         for _ in range(3):
-            part = rest.astype(BF16)
-            rest = rest - part.astype(F32)
-            both = jnp.dot(part[: MEMBERS // 2], fold_lo[...], preferred_element_type=F32)
-            both += jnp.dot(part[MEMBERS // 2 :], fold_hi[...], preferred_element_type=F32)
-            total = both if total is None else total + both
-        packed[t] = total
+            parts.append(rest.astype(BF16))
+            rest = rest - parts[-1].astype(F32)
+        h = MEMBERS // 2
+        low = jnp.concatenate([p[:h] for p in parts], axis=0)
+        high = jnp.concatenate([p[h:] for p in parts], axis=0)
+        both = jnp.dot(low, fold_lo[...], preferred_element_type=F32)
+        both += jnp.dot(high, fold_hi[...], preferred_element_type=F32)
+        packed[t] = both[:h] + both[h : 2 * h] + both[2 * h :]
 
     def swap(src, dst, send, recv, device):
         return pltpu.make_async_remote_copy(
@@ -387,30 +392,27 @@
             return [swap(packed.at[t, other], cbuf.at[t], c_sem.at[t, 0], c_sem.at[t, 1], at(dc=1))]
         if name == "back":
             return [swap(fin.at[t, own], fin.at[t, own], f_sem.at[t, 0], f_sem.at[t, 1], at(dc=1))]
-        src, buf, sem, key, count = {
-            "y": (ysrc, ybuf, y_sem, "dy", NY),
-            "x": (xsrc, xbuf, x_sem, "dx", NX),
-            "z": (zsrc, zbuf, z_sem, "dz", NZ),
-        }[name]
+        if name == "plane":
+            return [
+                swap(ysrc.at[t], ybuf.at[t, i], y_sem.at[t, i, 0], y_sem.at[t, i, 1], at(dy=dy, dx=dx))
+                for i, (dy, dx) in enumerate(PLANE)
+            ]
         return [
-            swap(src.at[t], buf.at[t, d - 1], sem.at[t, d - 1, 0], sem.at[t, d - 1, 1], at(**{key: d}))
-            for d in range(1, count)
+            swap(zsrc.at[t], zbuf.at[t, d - 1], z_sem.at[t, d - 1, 0], z_sem.at[t, d - 1, 1], at(dz=d))
+            for d in range(1, NZ)
         ]
 
-    def reduce_begin(t, between):
+    def reduce_begin(t, after_core, after_plane):
         pack(t)
         core = stage(t, "core")
         run(core)
+        after_core()
         core[0].wait()
         ysrc[t] = packed[t, own] + cbuf[t]
-        along = stage(t, "y")
-        run(along)
-        between(1)
-        collect(t, along, ysrc, ybuf, xsrc)
-        along = stage(t, "x")
-        run(along)
-        between(2)
-        collect(t, along, xsrc, xbuf, zsrc)
+        plane = stage(t, "plane")
+        run(plane)
+        after_plane()
+        collect(t, plane, ysrc, ybuf, zsrc)
         run(stage(t, "z"))
 
     def reduce_z(t):
@@ -445,7 +447,7 @@
 
     barrier = pltpu.get_barrier_semaphore()
     partners = [at(dc=1)]
-    partners += [at(dy=d) for d in (1, 2, 3)] + [at(dx=d) for d in (1, 2, 3)]
+    partners += [at(dy=dy, dx=dx) for dy, dx in PLANE]
     partners += [at(dz=d) for d in range(1, NZ)]
     for device in partners:
         pl.semaphore_signal(barrier, inc=1, device_id=device, device_id_type=MESH)
@@ -455,6 +457,8 @@
 
     for j in range(3):
         out1(0, j)
+    local(e_hbm, e_out, k_sem.at[0])
+    local(c_hbm, c_out, k_sem.at[1])
 
     @pl.when(jnp.logical_not(mine))
     def _():
@@ -482,11 +486,17 @@
     out1(1, 0)
     for j in range(3):
         arrived(0, j)
+        turn(j)
         gram(0, j, 0)
 
-    reduce_begin(0, lambda j: out1(1, j))
-    out2(1, 0)
+    def more_cotangent():
+        out2(1, 0)
+        out1(1, 2)
+
+    reduce_begin(0, lambda: out1(1, 1), more_cotangent)
     out2(1, 1)
+    arrived(1, 0)
+    gram(1, 0, 2)
     reduce_z(0)
     out2(1, 2)
     scores = scale * reduce_end(0)
@@ -504,14 +514,18 @@
 
     mix_branch(0)
     home1(0, 0)
-    mix_branch(1)
-    mix_branch(2)
-    for j in range(3):
+    for j in (1, 2):
         arrived(1, j)
         gram(1, j, 2)
 
-    reduce_begin(1, lambda j: home1(0, j))
-    home2(0, 0)
+    def more_branch():
+        home1(0, 1)
+        mix_branch(2)
+        home1(0, 2)
+        home2(0, 0)
+
+    reduce_begin(1, lambda: mix_branch(1), more_branch)
+    home2(0, 1)
     exp_b[...] = tn(wsave[...].astype(BF16), spread)
     blocks(tmat, (exp_b, 3))
     for j in range(3):
@@ -519,7 +533,6 @@
         for r in range(4):
             rows = slice(256 * r, 256 * r + 256)
             partial[j, rows, :] = jnp.dot(tmat[rows, :], right, preferred_element_type=F32)
-    home2(0, 1)
     reduce_z(1)
     home2(0, 2)
     pairs = reduce_end(1)
@@ -539,6 +552,8 @@
     for j in range(3):
         home2(1, j)
 
+    await_bytes(e_out, k_sem.at[0])
+    await_bytes(c_out, k_sem.at[1])
     for t in range(2):
         for sem in (s1_send, s2_send, q1_send, q2_send):
             await_bytes(ea1.at[pl.ds(0, 3)], sem.at[t, 0])
@@ -576,13 +591,14 @@
     square = lambda: pltpu.VMEM((ALL, ALL), BF16)
     small = lambda *lead: pltpu.VMEM((2,) + lead + (MEMBERS // 4, 2 * MEMBERS), F32)
     dma = pltpu.SemaphoreType.DMA
-    flat = jax.ShapeDtypeStruct((ROWS, CELL_DEV), BF16)
+    flat = pltpu.VMEM((ROWS, CELL_DEV), BF16)
+    vmem = pl.BlockSpec(memory_space=pltpu.VMEM)
     hbm = pl.BlockSpec(memory_space=pltpu.HBM)
-    branch, grad = pl.pallas_call(
+    branch, grad, ens, cot = pl.pallas_call(
         functools.partial(kernel, scale),
-        out_shape=(flat, flat),
+        out_shape=(flat,) * 4,
         in_specs=[hbm] * 6,
-        out_specs=(hbm, hbm),
+        out_specs=(vmem,) * 4,
         scratch_shapes=[pltpu.VMEM((4, CH, CH), BF16)]
         + [part() for _ in range(4)]
         + [full() for _ in range(4)]
@@ -590,16 +606,15 @@
         + [pltpu.VMEM((3, ALL, 2 * TILE), F32)]
         + [square() for _ in range(3)]
         + [
-            pltpu.VMEM((MEMBERS, ALL), F32),
+            pltpu.VMEM((3, 2 * TILE, ALL), BF16),
+            pltpu.VMEM((2, MEMBERS, ALL), F32),
             pltpu.VMEM((4, CH, 256), F32),
             pltpu.VMEM((ALL, 2 * MEMBERS), BF16),
             pltpu.VMEM((ALL, 2 * MEMBERS), BF16),
             pltpu.VMEM((2, MEMBERS // 2, 2 * MEMBERS), F32),
             small(),
             small(),
-            small(3),
-            small(),
-            small(3),
+            small(PEERS - 1),
             small(),
             small(NZ - 1),
             pltpu.VMEM((2, MEMBERS // 2, 2 * MEMBERS), F32),
@@ -609,6 +624,7 @@
         ]
         + [
             dma,
+            dma((2,)),
             dma((2, 2)),
             dma((2, 2, 3)),
             dma((2, 4, 4)),
@@ -618,8 +634,7 @@
             dma((2, 4)),
             dma((2,)),
             dma((2, 2)),
-            dma((2, 3, 2)),
-            dma((2, 3, 2)),
+            dma((2, PEERS - 1, 2)),
             dma((2, NZ - 1, 2)),
             dma((2, 2)),
             dma((2, 2)),
@@ -631,7 +646,7 @@
             dma((2,)),
         ],
         compiler_params=pltpu.CompilerParams(
-            collective_id=0, has_side_effects=True, vmem_limit_bytes=67043328
+            collective_id=0, has_side_effects=True, vmem_limit_bytes=67043328 - 4 * ROWS * CELL_DEV * 2
         ),
     )(
         ensemble.reshape(ROWS, CELL_DEV),
@@ -641,8 +656,8 @@
         w_value,
         w_out,
     )
-    updated = ensemble.astype(F32) + branch.reshape(shape).astype(F32)
-    ensemble_grad = cotangent.astype(F32) + grad.reshape(shape).astype(F32)
+    updated = ens.reshape(shape).astype(F32) + branch.reshape(shape).astype(F32)
+    ensemble_grad = cot.reshape(shape).astype(F32) + grad.reshape(shape).astype(F32)
     return updated, ensemble_grad
 
 

time: 98.8 us -> 94 us (0.951)
  other arithmetic: 5.85 us -> 3.14 us
  Pallas kernels: 92.2 us -> 90.1 us
    add x1, other arithmetic: 5.85 us -> 3.14 us  [shards(): cot.reshape(shape).astype(F32) + grad.reshape(shape).astype(F32)]
    pallas_call x1, Pallas kernels: 92.2 us -> 90.1 us  [shards(): pl.pallas_call(functools.partial(kernel, scale), out_shape=(flat,) * 4, i...]
where the time goes in v3:
time: 94 us; the launch traced here: 93.9 us
  Pallas kernels  90.1 us (96%)
  other arithmetic  3.14 us (3%)
    pallas_call x1, Pallas kernels, shards(): pl.pallas_call(functools.partial(kernel, scale), out_shape=(flat,) * 4, i...  90.1 us
    add x1, other arithmetic, shards(): cot.reshape(shape).astype(F32) + grad.reshape(shape).astype(F32)  3.14 us

profile of v3, /device:TPU:1, one launch (start us, length us, event | category | flops | bytes accessed | tf_op | source)
XLA Modules:
  0.0 93.9 jit_solution(13996849895457927421)
XLA Ops:
  0.6 90.1 %shard_map.77 = (bf16[64,11520]{1,0:T(8,128)(2,1)S(1)}, bf16[64,11520]{1,0:T(8,128)(2,1)S(1)}, bf16[64,11520]{1,0:T(8,128)(2,1)S(1)}, bf16[64,11520]{1,0:T(8,128)(2,1)S(1)}) custom-call(bf16[64,11520]{1,0:T(8,128)(2,1)} %bitcast.6, bf16[64,11520]{1,0:T(8,128)(2,1)} %bitcast.7, bf16[16,16]{1,0:T(8,128)(2,1)} %wq_hbm.1, bf16[16,16]{1,0:T(8,128)(2,1)} %wk_hbm.1, ...), custom_call_target="tpu_custom_call" | custom-call | tf_op jit(solution)/shard_map/pallas_call | solution.py:597
  90.8 3.1 %convert_add_fusion = (f32[64,11520]{1,0:T(8,128)}, f32[64,11520]{1,0:T(8,128)}) fusion(bf16[64,11520]{1,0:T(8,128)(2,1)S(1)} %get-tuple-element.9, bf16[64,11520]{1,0:T(8,128)(2,1)S(1)} %get-tuple-element.8, bf16[64,11520]{1,0:T(8,128)(2,1)S(1)} %get-tuple-element.7, bf16[64,11520]{1,0:T(8,128)(2,1)S(1)} %get-tuple-element.6), kind=kLoop, calls=%fused_computation | loop fusion | flops 4423680 | bytes 11796480 | tf_op jit(solution)/shard_map/add | solution.py:660

commit v4 on v3

--- a/solution.py
+++ b/solution.py
@@ -123,7 +123,7 @@
         )
 
     def more(yd, xd):
-        return 4 * lax.rem(xd + yd + 2 * c, 4) + yd
+        return 4 * lax.rem(xd + yd, 4) + lax.rem(yd + 2 * c, 4)
 
     def has_more(yd, xd):
         return more(yd, xd) < EXTRA
@@ -483,22 +483,23 @@
 
     for j in range(3):
         out2(0, j)
-    out1(1, 0)
     for j in range(3):
         arrived(0, j)
+        if j < 2:
+            out1(1, j)
         turn(j)
         gram(0, j, 0)
 
     def more_cotangent():
+        out1(1, 2)
         out2(1, 0)
-        out1(1, 2)
-
-    reduce_begin(0, lambda: out1(1, 1), more_cotangent)
+
+    reduce_begin(0, lambda: None, more_cotangent)
     out2(1, 1)
+    out2(1, 2)
+    reduce_z(0)
     arrived(1, 0)
     gram(1, 0, 2)
-    reduce_z(0)
-    out2(1, 2)
     scores = scale * reduce_end(0)
     exponent = jnp.exp(scores - jnp.max(scores, axis=1, keepdims=True))
     weights = exponent / jnp.sum(exponent, axis=1, keepdims=True)
@@ -514,18 +515,18 @@
 
     mix_branch(0)
     home1(0, 0)
-    for j in (1, 2):
-        arrived(1, j)
-        gram(1, j, 2)
+    arrived(1, 1)
+    gram(1, 1, 2)
+    mix_branch(1)
+    home1(0, 1)
+    arrived(1, 2)
+    gram(1, 2, 2)
 
     def more_branch():
-        home1(0, 1)
-        mix_branch(2)
+        home2(0, 0)
         home1(0, 2)
-        home2(0, 0)
-
-    reduce_begin(1, lambda: mix_branch(1), more_branch)
-    home2(0, 1)
+
+    reduce_begin(1, lambda: mix_branch(2), more_branch)
     exp_b[...] = tn(wsave[...].astype(BF16), spread)
     blocks(tmat, (exp_b, 3))
     for j in range(3):
@@ -533,6 +534,7 @@
         for r in range(4):
             rows = slice(256 * r, 256 * r + 256)
             partial[j, rows, :] = jnp.dot(tmat[rows, :], right, preferred_element_type=F32)
+    home2(0, 1)
     reduce_z(1)
     home2(0, 2)
     pairs = reduce_end(1)

time: 94 us -> 90.6 us (0.964)
  Pallas kernels: 90.1 us -> 86.7 us
    pallas_call x1, Pallas kernels: 90.1 us -> 86.7 us  [shards(): pl.pallas_call(functools.partial(kernel, scale), out_shape=(flat,) * 4, i...]
where the time goes in v4:
time: 90.6 us; the launch traced here: 90.5 us
  Pallas kernels  86.7 us (96%)
  other arithmetic  3.14 us (3%)
    pallas_call x1, Pallas kernels, shards(): pl.pallas_call(functools.partial(kernel, scale), out_shape=(flat,) * 4, i...  86.7 us
    add x1, other arithmetic, shards(): cot.reshape(shape).astype(F32) + grad.reshape(shape).astype(F32)  3.14 us

profile of v4, /device:TPU:1, one launch (start us, length us, event | category | flops | bytes accessed | tf_op | source)
XLA Modules:
  0.0 90.5 jit_solution(15944037099129243525)
XLA Ops:
  0.6 86.7 %shard_map.77 = (bf16[64,11520]{1,0:T(8,128)(2,1)S(1)}, bf16[64,11520]{1,0:T(8,128)(2,1)S(1)}, bf16[64,11520]{1,0:T(8,128)(2,1)S(1)}, bf16[64,11520]{1,0:T(8,128)(2,1)S(1)}) custom-call(bf16[64,11520]{1,0:T(8,128)(2,1)} %bitcast.6, bf16[64,11520]{1,0:T(8,128)(2,1)} %bitcast.7, bf16[16,16]{1,0:T(8,128)(2,1)} %wq_hbm.1, bf16[16,16]{1,0:T(8,128)(2,1)} %wk_hbm.1, ...), custom_call_target="tpu_custom_call" | custom-call | tf_op jit(solution)/shard_map/pallas_call | solution.py:599
  87.4 3.1 %convert_add_fusion = (f32[64,11520]{1,0:T(8,128)}, f32[64,11520]{1,0:T(8,128)}) fusion(bf16[64,11520]{1,0:T(8,128)(2,1)S(1)} %get-tuple-element.9, bf16[64,11520]{1,0:T(8,128)(2,1)S(1)} %get-tuple-element.8, bf16[64,11520]{1,0:T(8,128)(2,1)S(1)} %get-tuple-element.7, bf16[64,11520]{1,0:T(8,128)(2,1)S(1)} %get-tuple-element.6), kind=kLoop, calls=%fused_computation | loop fusion | flops 4423680 | bytes 11796480 | tf_op jit(solution)/shard_map/add | solution.py:662

commit v5 on v4

--- a/solution.py
+++ b/solution.py
@@ -335,6 +335,21 @@
         for q in range(4):
             turned[j, :, 256 * q : 256 * q + 256] = cells(0, j, q).T
 
+    sub = lax.broadcasted_iota(jnp.int32, (1, 8, 256), 1)
+
+    def fold_rows(s):
+        v = (s[:, :8] + s[:, 8:]).reshape(2, 2, 4, 8, 256)
+        a, b = v[:, 0].reshape(8, 8, 256), v[:, 1].reshape(8, 8, 256)
+        low = sub < 4
+        v = jnp.where(low, a, b) + pltpu.roll(jnp.where(low, b, a), 4, 1)
+        for width in (2, 1):
+            v = v.reshape(2, 2, width, 8, 256)
+            a, b = v[:, 0].reshape(2 * width, 8, 256), v[:, 1].reshape(2 * width, 8, 256)
+            v = jnp.where(
+                lax.rem(sub, 2 * width) < width, a + pltpu.roll(a, 8 - width, 1), b + pltpu.roll(b, width, 1)
+            )
+        return v.reshape(CH, 256)
+
     def gram(t, j, const):
         @pl.loop(0, 4)
         def _(r):
@@ -344,7 +359,7 @@
                 cols = slice(256 * q, 256 * q + 256)
                 s = jnp.dot(left, turned[j, :, cols], preferred_element_type=F32)
                 s = s.reshape(CH, CH, 256) * consts[const][None]
-                s = jnp.sum(s, axis=1)
+                s = fold_rows(s)
                 if j == 0:
                     acc[t, rows, cols] = s
                 else:

time: 90.6 us -> 90 us (level)
  no operation moved by 1% of the time
where the time goes in v5:
time: 90 us
  Pallas kernels  86.2 us (96%)
  other arithmetic  3.14 us (3%)
    pallas_call x1, Pallas kernels, shards(): pl.pallas_call(functools.partial(kernel, scale), out_shape=(flat,) * 4, i...  86.2 us
    add x1, other arithmetic, shards(): cot.reshape(shape).astype(F32) + grad.reshape(shape).astype(F32)  3.14 us

profile of v5, /device:TPU:1, one launch (start us, length us, event | category | flops | bytes accessed | tf_op | source)
XLA Modules:
  0.0 90.0 jit_solution(8807168161516021729)
XLA Ops:
  0.6 86.2 %shard_map.77 = (bf16[64,11520]{1,0:T(8,128)(2,1)S(1)}, bf16[64,11520]{1,0:T(8,128)(2,1)S(1)}, bf16[64,11520]{1,0:T(8,128)(2,1)S(1)}, bf16[64,11520]{1,0:T(8,128)(2,1)S(1)}) custom-call(bf16[64,11520]{1,0:T(8,128)(2,1)} %bitcast.6, bf16[64,11520]{1,0:T(8,128)(2,1)} %bitcast.7, bf16[16,16]{1,0:T(8,128)(2,1)} %wq_hbm.1, bf16[16,16]{1,0:T(8,128)(2,1)} %wk_hbm.1, ...), custom_call_target="tpu_custom_call" | custom-call | tf_op jit(solution)/shard_map/pallas_call | solution.py:614
  86.8 3.1 %convert_add_fusion = (f32[64,11520]{1,0:T(8,128)}, f32[64,11520]{1,0:T(8,128)}) fusion(bf16[64,11520]{1,0:T(8,128)(2,1)S(1)} %get-tuple-element.9, bf16[64,11520]{1,0:T(8,128)(2,1)S(1)} %get-tuple-element.8, bf16[64,11520]{1,0:T(8,128)(2,1)S(1)} %get-tuple-element.7, bf16[64,11520]{1,0:T(8,128)(2,1)S(1)} %get-tuple-element.6), kind=kLoop, calls=%fused_computation | loop fusion | flops 4423680 | bytes 11796480 | tf_op jit(solution)/shard_map/add | solution.py:677

commit v6 on v5

--- a/solution.py
+++ b/solution.py
@@ -351,7 +351,7 @@
         return v.reshape(CH, 256)
 
     def gram(t, j, const):
-        @pl.loop(0, 4)
+        @pl.loop(0, 4, unroll=2)
         def _(r):
             rows = pl.ds(pl.multiple_of(r * CH, CH), CH)
             left = cells(t, j, r)
@@ -444,7 +444,7 @@
     ).astype(BF16)
 
     def blocks(dst, *terms):
-        @pl.loop(0, MEMBERS)
+        @pl.loop(0, MEMBERS, unroll=4)
         def _(m):
             rows = pl.ds(pl.multiple_of(m * CH, CH), CH)
             for q in range(4):

time: 90 us -> 89.7 us (level)
  no operation moved by 1% of the time
where the time goes in v6:
time: 89.7 us; the launch traced here: 89.6 us
  Pallas kernels  85.8 us (96%)
  other arithmetic  3.14 us (4%)
    pallas_call x1, Pallas kernels, shards(): pl.pallas_call(functools.partial(kernel, scale), out_shape=(flat,) * 4, i...  85.8 us
    add x1, other arithmetic, shards(): cot.reshape(shape).astype(F32) + grad.reshape(shape).astype(F32)  3.14 us

profile of v6, /device:TPU:1, one launch (start us, length us, event | category | flops | bytes accessed | tf_op | source)
XLA Modules:
  0.0 89.6 jit_solution(21453731226671577)
XLA Ops:
  0.6 85.8 %shard_map.77 = (bf16[64,11520]{1,0:T(8,128)(2,1)S(1)}, bf16[64,11520]{1,0:T(8,128)(2,1)S(1)}, bf16[64,11520]{1,0:T(8,128)(2,1)S(1)}, bf16[64,11520]{1,0:T(8,128)(2,1)S(1)}) custom-call(bf16[64,11520]{1,0:T(8,128)(2,1)} %bitcast.6, bf16[64,11520]{1,0:T(8,128)(2,1)} %bitcast.7, bf16[16,16]{1,0:T(8,128)(2,1)} %wq_hbm.1, bf16[16,16]{1,0:T(8,128)(2,1)} %wk_hbm.1, ...), custom_call_target="tpu_custom_call" | custom-call | tf_op jit(solution)/shard_map/pallas_call | solution.py:614
  86.5 3.1 %convert_add_fusion = (f32[64,11520]{1,0:T(8,128)}, f32[64,11520]{1,0:T(8,128)}) fusion(bf16[64,11520]{1,0:T(8,128)(2,1)S(1)} %get-tuple-element.9, bf16[64,11520]{1,0:T(8,128)(2,1)S(1)} %get-tuple-element.8, bf16[64,11520]{1,0:T(8,128)(2,1)S(1)} %get-tuple-element.7, bf16[64,11520]{1,0:T(8,128)(2,1)S(1)} %get-tuple-element.6), kind=kLoop, calls=%fused_computation | loop fusion | flops 4423680 | bytes 11796480 | tf_op jit(solution)/shard_map/add | solution.py:677
